TPU v7x, 256 devices: a whole 4x4x8 slice. The times are simulated.
256 devices in a mesh: gx: 8 (over y, core), gy: 32 (over x, z).
Axes of the slice: x: 4, y: 4, z: 8, core: 2. Of those that a mesh axis runs over, the one named last changes fastest.
Arguments:
- projected: bfloat16 [32, 512, 3072], P('gx', 'gy'), may hold values from -8 to 8
- residual: bfloat16 [32, 512, 1024], P('gx', 'gy'), may hold values from -6 to 6
- page_store: bfloat16 [256, 72, 128, 256], P(('gx', 'gy')), may hold values from -8 to 8
- page_table: int32 [32, 64], P('gx'), may hold values from 0 to 71, as said below
- lengths: int32 [32], P('gx'), may hold values from 1 to 8192, as said below
- persistent: bfloat16 [2, 16, 1024], replicated, may hold values from -8 to 8
- memory_rates: float32 [256, 3, 8], P(('gx', 'gy')), may hold values from 0.002 to 0.95
- memory_state: float32 [256, 128, 128], P(('gx', 'gy')), may hold values from -6 to 6
- momentum: float32 [256, 128, 128], P(('gx', 'gy')), may hold values from -2 to 2
- w_out: bfloat16 [1024, 1024], P('gy', 'gx'), may hold values from -0.1875 to 0.1875
Outputs:
- layer_out: bfloat16 [32, 512, 1024], P('gx', 'gy')
- memory_next: float32 [256, 128, 128], P(('gx', 'gy'))
- momentum_next: float32 [256, 128, 128], P(('gx', 'gy'))
Inputs may be any that keep to these rules, and one draw needn't show every extreme that they name: `page_table`: the 64 entries of a request's row are distinct slots. `lengths`: some request has exactly 8192 cached tokens.
All inputs are finite; a program needn't handle non-finite values.
Results may differ from a plain program's by a relative error of at most 0.012.
Values may be sent and summed in bfloat16 or wider, within the bound.
No kernel may reach another device: no remote copies, remote signals or barrier semaphores. Data moves between devices by JAX's collectives and lax.ppermute only.
A program may use at most 64 MiB of HBM per device.

v0:
```python
import math

import jax
import jax.numpy as jnp
from jax import lax
from jax.sharding import PartitionSpec as P

D = 1024
HEADS = 8
HD = 128
MB = 64
PAGE = 128
MAXP = 64
NB = 8


masked_score = -1e30


def for_sending(value):

    def short(part):
        return part.astype(jnp.bfloat16) if part.dtype == jnp.float32 else part

    return jax.tree.map(short, value)


def absorb(carried, scores, values):
    running, totals, summed = carried
    newest = jnp.maximum(running, jnp.max(scores, axis=1))
    factor = jnp.exp(running - newest)
    weights = jnp.exp(scores - newest[:, None])
    totals = totals * factor + jnp.sum(weights, axis=1)
    summed = summed * factor[:, None] + jnp.dot(
        weights.astype(jnp.bfloat16), values, preferred_element_type=jnp.float32
    )
    return (newest, totals, summed)


def recall(queries, keyed, valued, rates_here, memory, moment):
    keys_wide = keyed.astype(jnp.float32)
    keys_wide = keys_wide / jnp.sqrt(jnp.sum(keys_wide * keys_wide, axis=1, keepdims=True) + 1e-06)
    query_wide = queries.astype(jnp.float32)
    query_wide = query_wide / jnp.sqrt(
        jnp.sum(query_wide * query_wide, axis=1, keepdims=True) + 1e-06
    )
    values_wide = valued.astype(jnp.float32)
    pieces = []
    for block_id in range(NB):
        start_row = block_id * MB
        key_block = keys_wide[start_row : start_row + MB]
        query_block = query_wide[start_row : start_row + MB]
        value_block = values_wide[start_row : start_row + MB]
        pieces.append(jnp.dot(query_block, memory, precision=lax.Precision.HIGHEST))
        errors = jnp.dot(key_block, memory, precision=lax.Precision.HIGHEST) - value_block
        gradient = jnp.dot(key_block.T, errors, precision=lax.Precision.HIGHEST)
        moment = rates_here[0, block_id] * moment - rates_here[1, block_id] * gradient
        memory = (1.0 - rates_here[2, block_id]) * memory + moment
    return (jnp.concatenate(pieces, 0), memory, moment)


def shards(
    projected,
    residual,
    page_store,
    page_table,
    lengths,
    persistent,
    memory_rates,
    memory_state,
    momentum,
    w_out,
):
    groups, positions, triple = projected.shape
    pair_count = memory_state.shape[0]
    sectioned = (
        projected.reshape(groups, positions, 3, HEADS, HD)
        .transpose(0, 3, 1, 2, 4)
        .reshape(groups * HEADS, positions, 3 * HD)
    )
    paired = lax.all_to_all(sectioned, "gy", split_axis=0, concat_axis=1, tiled=True)
    offset = lax.axis_index("gy") * pair_count
    pages_block = math.gcd(MAXP, max(1, 512 // PAGE))
    key_span = pages_block * PAGE
    scaling = HD ** (-0.5)

    def handle(member):
        ordinal, segment, pages_here, rates_here, memory, moment = member
        within = offset + ordinal
        request = within // HEADS
        head_id = within % HEADS
        table_row = lax.dynamic_index_in_dim(page_table, request, 0, keepdims=False)
        length = lax.dynamic_index_in_dim(lengths, request, 0, keepdims=False)
        pers_keys = lax.dynamic_slice_in_dim(persistent[0], head_id * HD, HD, 1)
        pers_values = lax.dynamic_slice_in_dim(persistent[1], head_id * HD, HD, 1)
        queries = segment[:, :HD]
        keyed = segment[:, HD : 2 * HD]
        valued = segment[:, 2 * HD :]
        row_count = segment.shape[0]
        carried = (
            jnp.full((row_count,), masked_score, jnp.float32),
            jnp.zeros((row_count,), jnp.float32),
            jnp.zeros((row_count, HD), jnp.float32),
        )
        scores = jnp.dot(queries, pers_keys.T, preferred_element_type=jnp.float32) * scaling
        carried = absorb(carried, scores, pers_values)

        def visit_block(block_id, carried):
            first_page = block_id * pages_block
            fetched_pages = []
            for within_block in range(pages_block):
                slot_here = lax.dynamic_index_in_dim(
                    table_row, first_page + within_block, 0, keepdims=False
                )
                fetched_pages.append(
                    lax.dynamic_index_in_dim(pages_here, slot_here, 0, keepdims=False)
                )
            fetched = jnp.concatenate(fetched_pages, 0)
            key_pos = block_id * key_span + jnp.arange(key_span, dtype=jnp.int32)
            scores = (
                jnp.dot(queries, fetched[:, :HD].T, preferred_element_type=jnp.float32) * scaling
            )
            scores = jnp.where((key_pos < length)[None, :], scores, masked_score)
            return absorb(carried, scores, fetched[:, HD:])

        block_count = MAXP // pages_block
        carried = lax.fori_loop(0, block_count, visit_block, carried)
        places = jnp.arange(row_count, dtype=jnp.int32)
        causal = places[None, :] <= places[:, None]
        scores = jnp.dot(queries, keyed.T, preferred_element_type=jnp.float32) * scaling
        scores = jnp.where(causal, scores, masked_score)
        newest, totals, summed = absorb(carried, scores, valued)
        attended = summed / totals[:, None]
        recalled, memory, moment = recall(queries, keyed, valued, rates_here, memory, moment)
        mixed = (attended + recalled).astype(jnp.bfloat16)
        return (mixed, memory, moment)

    mixed, memory_next, momentum_next = lax.map(
        handle,
        (
            jnp.arange(pair_count, dtype=jnp.int32),
            paired,
            page_store,
            memory_rates,
            memory_state,
            momentum,
        ),
    )
    returned = jax.tree.map(
        lambda part, own: part.astype(own.dtype),
        lax.all_to_all(for_sending(mixed), "gy", split_axis=1, concat_axis=0, tiled=True),
        mixed,
    )
    tokens_here = (
        returned.reshape(groups, HEADS, positions, HD)
        .transpose(0, 2, 1, 3)
        .reshape(groups, positions, D)
    )
    wide_rows = lax.all_gather(w_out, "gx", axis=1, tiled=True)
    flattened = tokens_here.reshape(groups * positions, D)
    weight_piece = lax.all_gather(wide_rows, "gy", axis=0, tiled=True)
    taken = lax.slice_in_dim(flattened, 0, weight_piece.shape[0], axis=1)
    product = jnp.zeros((groups * positions, D), jnp.float32) + jnp.dot(
        taken, weight_piece, preferred_element_type=jnp.float32
    )
    layer_out = (
        (residual.reshape(groups * positions, D).astype(jnp.float32) + product)
        .astype(jnp.bfloat16)
        .reshape(groups, positions, D)
    )
    return (layer_out, memory_next, momentum_next)


def solution(mesh):
    in_specs = (
        P("gx", "gy", None),
        P("gx", "gy", None),
        P(("gx", "gy"), None, None, None),
        P("gx", None),
        P("gx"),
        P(),
        P(("gx", "gy"), None, None),
        P(("gx", "gy"), None, None),
        P(("gx", "gy"), None, None),
        P("gy", "gx"),
    )
    out_specs = (P("gx", "gy", None), P(("gx", "gy"), None, None), P(("gx", "gy"), None, None))
    return jax.shard_map(shards, mesh=mesh, in_specs=in_specs, out_specs=out_specs, check_vma=False)
```

profile of v0, /device:TPU:1, one launch (start us, length us, event | category | flops | bytes accessed | tf_op | source)
XLA Modules:
  0.0 269.6 jit_solution(14022602897338889470)
XLA Ops:
  7.2 1.1 copy.24
  8.6 1.1 reshape.79
  9.7 12.0 %all-to-all-start = ((bf16[32,16,384]{2,1,0:T(8,128)(2,1)}), bf16[32,16,384]{2,1,0:T(8,128)(2,1)S(1)}, u32[]{:S(2)}, u32[]{:S(2)}) async-start(bf16[32,16,384]{2,1,0:T(8,128)(2,1)} %reshape.79), calls=%async_computation | async-start | bytes 786432 | tf_op jit(solution)/shard_map/all_to_all | solution.py:81
  21.7 13.9 %all_gather.6 = bf16[32,1024]{1,0:T(8,128)(2,1)} all-gather(bf16[32,128]{1,0:T(8,128)(2,1)S(1)} %copy-done.6), channel_id=1, replica_groups=mesh['gx'=8,'gy'=32] {'gx'}, dimensions={1}, use_global_device_ids=true | all-gather | bytes 73728 | tf_op jit(solution)/shard_map/all_gather | solution.py:159
  37.5 0.7 fusion.76
  43.8 1.5 fusion.33
  45.5 1.6 multiply_add_fusion.6
  47.8 180.2 %while.30 = (s32[]{:T(128)}, f32[512]{0:T(512)S(1)}, f32[512]{0:T(512)S(1)}, f32[512,128]{1,0:T(8,128)S(1)}, s32[]{:T(128)}, /*index=5*/s32[64]{0:T(128)S(1)}, b...) while((s32[]{:T(128)}, f32[512]{0:T(512)S(1)}, ...), condition=%wide.region_5.6_spmd, body=%wide.region_2.5_spmd.sunk | while | flops 137234464 | bytes 5146177 | solution.py:127
  56.4 1.0 dynamic-slice_bitcast_fusion.5
  57.4 0.7 add_compare_fusion.2
  67.6 1.0 dynamic-slice_bitcast_fusion.5
  68.6 0.7 add_compare_fusion.2
  78.9 1.0 dynamic-slice_bitcast_fusion.5
  79.9 0.7 add_compare_fusion.2
  90.2 1.0 dynamic-slice_bitcast_fusion.5
  91.2 0.7 add_compare_fusion.2
  101.4 1.0 dynamic-slice_bitcast_fusion.5
  102.4 0.7 add_compare_fusion.2
  112.7 1.0 dynamic-slice_bitcast_fusion.5
  113.7 0.7 add_compare_fusion.2
  124.0 1.0 dynamic-slice_bitcast_fusion.5
  125.0 0.7 add_compare_fusion.2
  135.2 1.0 dynamic-slice_bitcast_fusion.5
  136.2 0.7 add_compare_fusion.2
  146.5 1.0 dynamic-slice_bitcast_fusion.5
  147.5 0.7 add_compare_fusion.2
  157.7 1.0 dynamic-slice_bitcast_fusion.5
  158.7 0.7 add_compare_fusion.2
  169.0 1.0 dynamic-slice_bitcast_fusion.5
  170.0 0.7 add_compare_fusion.2
  180.3 1.0 dynamic-slice_bitcast_fusion.5
  191.5 1.0 dynamic-slice_bitcast_fusion.5
  202.8 1.0 dynamic-slice_bitcast_fusion.5
  203.8 0.7 add_compare_fusion.2
  214.1 1.0 dynamic-slice_bitcast_fusion.5
  215.1 0.7 add_compare_fusion.2
  225.3 1.0 dynamic-slice_bitcast_fusion.5
  226.3 0.7 add_compare_fusion.2
  228.8 1.5 multiply_add_fusion.5
  230.7 1.5 multiply_add_fusion.4
  232.5 1.6 multiply_add_fusion.3
  234.5 1.4 multiply_add_fusion.2
  236.3 1.5 multiply_add_fusion.1
  239.1 1.4 reduce.4
  241.2 9.5 %all-to-all-start.1 = ((bf16[32,2,1024]{2,1,0:T(2,128)(2,1)}), bf16[32,2,1024]{2,1,0:T(2,128)(2,1)S(1)}, u32[]{:S(2)}, u32[]{:S(2)}) async-start(bf16[32,2,1024]{2,1,0:T(2,128)(2,1)} %reshape.83), calls=%async_computation.1 | async-start | bytes 262144 | tf_op jit(solution)/shard_map/all_to_all | solution.py:151
  250.9 1.5 fusion.13
  253.1 6.7 %all-to-all-done.1 = bf16[32,2,1024]{2,1,0:T(2,128)(2,1)S(1)} async-done(((bf16[32,2,1024]{2,1,0:T(2,128)(2,1)}), bf16[32,2,1024]{2,1,0:T(2,128)(2,1)S(1)}, u32[]{:S(2)}, u32[]{:S(2)}) %all-to-all-start.1) | async-done | bytes 131104 | tf_op jit(solution)/shard_map/all_to_all | solution.py:151
  260.1 2.7 %fusion.10 = bf16[64,1024]{1,0:T(8,128)(2,1)} fusion(bf16[1024,1024]{1,0:T(8,128)(2,1)} %all-gather.2.cloned.1.call-done, bf16[64,1024]{1,0:T(8,128)(2,1)S(1)} %bitcast.140, bf16[8,8,8,128]{3,2,1,0:T(8,128)(2,1)S(1)} %bitcast.135), kind=kOutput, calls=%fused_computation.24 | convolution fusion | flops 134414336 | bytes 2490368 | tf_op jit(solution)/shard_map/dot_general | solution.py:163
  (195 shorter events, 36.3 us)
Async XLA Ops:
  7.2 35.6 %copy-start = (s32[4,64]{1,0:T(4,128)S(1)}, s32[4,64]{1,0:T(4,128)}, u32[]{:S(2)}) copy-start(s32[4,64]{1,0:T(4,128)} %param.15) | copy-start | bytes 3076
  7.2 14.6 %copy-start.6 = (bf16[32,128]{1,0:T(8,128)(2,1)S(1)}, bf16[32,128]{1,0:T(8,128)(2,1)}, u32[]{:S(2)}) copy-start(bf16[32,128]{1,0:T(8,128)(2,1)} %param.21) | copy-start | bytes 24580
  7.2 28.5 %copy-start.7 = (f32[1,3,8]{2,0,1:T(1,128)S(1)}, f32[1,3,8]{2,0,1:T(1,128)}, u32[]{:S(2)}) copy-start(f32[1,3,8]{2,0,1:T(1,128)} %param.18) | copy-start | bytes 292
  7.2 34.9 %copy-start.8 = (s32[4]{0:T(128)S(1)}, s32[4]{0:T(128)}, u32[]{:S(2)}) copy-start(s32[4]{0:T(128)} %param.16) | copy-start | bytes 52
  7.2 35.5 %copy-start.5 = (bf16[2,16,1024]{2,1,0:T(8,128)(2,1)S(1)}, bf16[2,16,1024]{2,1,0:T(8,128)(2,1)}, u32[]{:S(2)}) copy-start(bf16[2,16,1024]{2,1,0:T(8,128)(2,1)} %param.17) | copy-start | bytes 196612
  9.7 33.9 %copy-start.1 = (f32[1,128,128]{2,1,0:T(8,128)S(1)}, f32[1,128,128]{2,1,0:T(8,128)}, u32[]{:S(2)}) copy-start(f32[1,128,128]{2,1,0:T(8,128)} %param.19) | copy-start | bytes 196612
  9.7 33.1 %all-to-all-start = ((bf16[32,16,384]{2,1,0:T(8,128)(2,1)}), bf16[32,16,384]{2,1,0:T(8,128)(2,1)S(1)}, u32[]{:S(2)}, u32[]{:S(2)}) async-start(bf16[32,16,384]{2,1,0:T(8,128)(2,1)} %reshape.79), calls=%async_computation | async-start | bytes 786432 | tf_op jit(solution)/shard_map/all_to_all | solution.py:81
  21.7 22.1 %copy-start.4 = (f32[1,128,128]{2,1,0:T(8,128)S(1)}, f32[1,128,128]{2,1,0:T(8,128)}, u32[]{:S(2)}) copy-start(f32[1,128,128]{2,1,0:T(8,128)} %param.20) | copy-start | bytes 196612
  21.7 238.4 %all-gather.2.cloned.1.call-start = ((), (), s32[]{:S(2)}) async-start(), calls=%async_computation.2 | async-start | bytes 2162688 | tf_op jit(solution)/shard_map/all_gather | solution.py:161
  238.0 22.1 %copy-start.3 = (bf16[4,16,1024]{2,1,0:T(8,128)(2,1)S(1)}, bf16[4,16,1024]{2,1,0:T(8,128)(2,1)}, u32[]{:S(2)}) copy-start(bf16[4,16,1024]{2,1,0:T(8,128)(2,1)} %param.13) | copy-start | bytes 393220
  241.2 18.6 %all-to-all-start.1 = ((bf16[32,2,1024]{2,1,0:T(2,128)(2,1)}), bf16[32,2,1024]{2,1,0:T(2,128)(2,1)S(1)}, u32[]{:S(2)}, u32[]{:S(2)}) async-start(bf16[32,2,1024]{2,1,0:T(2,128)(2,1)} %reshape.83), calls=%async_computation.1 | async-start | bytes 262144 | tf_op jit(solution)/shard_map/all_to_all | solution.py:151
  252.4 10.4 %copy-start.2 = (f32[128,128]{1,0:T(8,128)}, f32[128,128]{1,0:T(8,128)S(1)}, u32[]{:S(2)}) copy-start(f32[128,128]{1,0:T(8,128)S(1)} %fusion.13) | copy-start | bytes 196612
Sparse Core Ops, SparseCore 0:
  35.8 73.8 all-gather.1
where the time goes:
time: 273 us; the launch traced here: 270 us
  loops' own time  127 us (47%)
  local copies, waits for them, and re-layouts  32.4 us (12%)
  matrix products  30.4 us (11%)
  starting transfers between devices  21.5 us (8%)
  between operations  19.5 us (7%)
  other arithmetic  17.8 us (7%)
  blocking collectives  13.9 us (5%)
  waiting for transfers between devices  6.78 us (2%)
    another operation x1, loops' own time, handle(): carried = lax.fori_loop(0, block_count, visit_block, carried)  127 us
    squeeze x16, local copies, waits for them, and re-layouts, visit_block(): lax.dynamic_index_in_dim(pages_here, slot_here, 0, keepdims=False)  15.4 us
    all_gather x1, blocking collectives, shards(): wide_rows = lax.all_gather(w_out, 'gx', axis=1, tiled=True)  13.9 us
    dot_general x8, matrix products, recall(): gradient = jnp.dot(key_block.T, errors, precision=lax.Precision.HIGHEST)  12.1 us
    all_to_all x1, starting transfers between devices, shards(): lax.all_to_all(sectioned, 'gy', split_axis=0, concat_axis=1, tiled=True)  12 us
    lt x16, other arithmetic, visit_block(): scores = jnp.where((key_pos < length)[None, :], scores, masked_score)  11.1 us
    dynamic_slice x16, local copies, waits for them, and re-layouts, visit_block(): lax.dynamic_index_in_dim(table_row, first_page + within_block, 0, keepdim...  10.9 us
    all_to_all x1, starting transfers between devices, shards(): lax.all_to_all(for_sending(mixed), 'gy', split_axis=1, concat_axis=0, til...  9.47 us
  transfers between devices with their start and end apart: 3, of which 1 were waited for; matrix products, arithmetic and copies ran while one was open for 28% of the time, Pallas kernels for 0%

commit v1 on v0

v1 whole, which is shorter than its diff:
```python
import math

import jax
import jax.numpy as jnp
from jax import lax
from jax.experimental import pallas as pl
from jax.experimental.pallas import tpu as pltpu
from jax.sharding import PartitionSpec as P

D, HEADS, HD, MB, PAGE, MAXP, NB, PERSIST = 1024, 8, 128, 64, 128, 64, 8, 16
ROWS = 512
SPAN = 1024
PPB = SPAN // PAGE
BLOCKS = MAXP // PPB
LEAD = 128
POOL, CHUNK = 72, 9
SCALE = HD ** (-0.5) * math.log2(math.e)
LOW = -1e30
bf, f32 = jnp.bfloat16, jnp.float32


def halves(x):
    high = x.astype(bf)
    return high, (x - high.astype(f32)).astype(bf)


def contract_rows(a, b):
    return lax.dot_general(a, b, (((0,), (0,)), ((), ())), preferred_element_type=f32)


def contract_lanes(a, b):
    return lax.dot_general(a, b, (((1,), (1,)), ((), ())), preferred_element_type=f32)


def unit_rows(x):
    high, low = halves(x * x)
    squares = jnp.dot(
        jnp.concatenate([high, low], 1), jnp.ones((2 * HD, HD), bf), preferred_element_type=f32
    )
    return x * lax.rsqrt(squares + 1e-06)


def pair_kernel(
    table_hbm, lengths_hbm, rates_hbm, arrived, persistent, memory_in, moment_in, pages_hbm,
    mixed, memory_out, moment_out,
    table, lengths, rates, qkv, pages, query2, lead, scores_a, scores_b, top, sums, left, right, recalled, sems,
):
    member = lax.axis_index("gy")
    request, head = member // HEADS, lax.rem(member, HEADS)
    columns = pl.ds(pl.multiple_of(head * HD, HD), HD)
    moves = [
        (arrived.at[:, : 3 * HD], qkv),
        (persistent.at[0, :, columns], lead.at[:PERSIST, :HD]),
        (persistent.at[1, :, columns], lead.at[:PERSIST, HD:]),
        (table_hbm, table),
        (lengths_hbm, lengths),
        (rates_hbm, rates),
        (memory_in, memory_out),
        (moment_in, moment_out),
    ] + [
        (pages_hbm.at[0, pl.ds(i, CHUNK)], pages.at[pl.ds(i, CHUNK)]) for i in range(0, POOL, CHUNK)
    ]
    copies = [pltpu.make_async_copy(a, b, sems.at[i]) for i, (a, b) in enumerate(moves)]
    for copy in copies:
        copy.start()
    copies[0].wait()

    queries = qkv[:, :HD].astype(f32)
    high, low = halves(queries * SCALE)
    query2[:, :HD] = high
    query2[:, HD:] = low

    qh, ql = halves(unit_rows(queries))
    kh, kl = halves(unit_rows(qkv[:, HD : 2 * HD].astype(f32)))
    valued = qkv[:, 2 * HD : 3 * HD]
    nothing = jnp.zeros((MB, HD), bf)
    for b in range(NB):
        r = slice(b * MB, (b + 1) * MB)
        one = jnp.concatenate([kh[r], kh[r], kl[r]], 0)
        two = jnp.concatenate(
            [
                jnp.concatenate([kh[r], valued[r]], 1),
                jnp.concatenate([kl[r], nothing], 1),
                jnp.concatenate([kh[r], valued[r]], 1),
            ],
            0,
        )
        both = contract_rows(one, two)
        gh, gl = halves(both[:, :HD])
        left[b, :HD, :] = jnp.concatenate([gh, gl, gh], 1)
        left[b, HD:, :] = jnp.concatenate([qh[r], ql[r], qh[r]], 1)
        right[b] = both[:, HD:]

    def memory_step(b):
        memory = memory_out[0]
        mh, ml = halves(memory)
        product = jnp.dot(left[b], jnp.concatenate([mh, mh, ml], 0), preferred_element_type=f32)
        recalled[pl.ds(pl.multiple_of(b * MB, MB), MB), :] = product[HD:]
        moment = rates[0, 0, b] * moment_out[0] - rates[1, 0, b] * (product[:HD] - right[b])
        moment_out[0] = moment
        memory_out[0] = (1.0 - rates[2, 0, b]) * memory + moment

    copies[1].wait()
    copies[2].wait()
    lead[PERSIST:LEAD, :] = jnp.zeros((LEAD - PERSIST, 2 * HD), bf)
    lead[LEAD:, :] = qkv[:, HD : 3 * HD]
    width = LEAD + ROWS
    first = contract_lanes(query2[...], jnp.concatenate([lead[:, :HD]] * 2, 1))
    row = lax.broadcasted_iota(jnp.int32, (ROWS, width), 0)
    col = lax.broadcasted_iota(jnp.int32, (ROWS, width), 1)
    allowed = (col < PERSIST) | ((col >= LEAD) & (col <= row + LEAD))
    first = jnp.where(allowed, first, LOW)
    peak = jnp.broadcast_to(jnp.max(first, axis=1, keepdims=True), (ROWS, HD))
    top[...] = peak
    weights = jnp.exp2(first - peak[:, :1])
    ones = jnp.ones((width, HD), bf)
    sums[...] = jnp.dot(
        weights.astype(bf), jnp.concatenate([lead[:, HD:], ones], 1), preferred_element_type=f32
    )
    for copy in copies[3:]:
        copy.wait()
    length = lengths[request]

    def page_of(b, columns):
        return jnp.concatenate(
            [pages[table[request, jnp.minimum(b * PPB + i, MAXP - 1)], :, columns] for i in range(PPB)], 0
        )

    def score(b, scores):
        keys = page_of(b, slice(0, HD))
        place = lax.broadcasted_iota(jnp.int32, (1, SPAN), 1) + b * SPAN
        bias = jnp.where(place < length, 0.0, LOW).astype(f32)
        scores[...] = contract_lanes(query2[...], jnp.concatenate([keys, keys], 1)) + bias

    def absorb(b, scores):
        values = jnp.concatenate([page_of(b, slice(HD, 2 * HD)), jnp.ones((SPAN, HD), bf)], 1)
        before = top[...]
        peak = jnp.maximum(before, jnp.max(scores[...], axis=1, keepdims=True))
        top[...] = peak
        factor = jnp.exp2(before - peak)
        weights = jnp.exp2(scores[...] - peak[:, :1]).astype(bf)
        added = jnp.dot(weights, values, preferred_element_type=f32)
        sums[...] = sums[...] * jnp.concatenate([factor, factor], 1) + added

    score(0, scores_a)
    twos = (length + 2 * SPAN - 1) // (2 * SPAN)

    def two_blocks(i, carry):
        score(2 * i + 1, scores_b)
        absorb(2 * i, scores_a)
        memory_step(2 * i)
        score(2 * i + 2, scores_a)
        absorb(2 * i + 1, scores_b)
        memory_step(2 * i + 1)
        return carry

    lax.fori_loop(0, twos, two_blocks, 0)

    def rest(b, carry):
        memory_step(b)
        return carry

    lax.fori_loop(2 * twos, NB, rest, 0)
    mixed[...] = (sums[:, :HD] / sums[:, HD:] + recalled[...]).astype(bf)


def pair_call(table, lengths, rates, arrived, persistent, memory, moment, pages):
    hbm = pl.BlockSpec(memory_space=pltpu.HBM)
    vmem = pl.BlockSpec(memory_space=pltpu.VMEM)
    return pl.pallas_call(
        pair_kernel,
        out_shape=(
            jax.ShapeDtypeStruct((ROWS, HD), bf),
            jax.ShapeDtypeStruct((1, HD, HD), f32),
            jax.ShapeDtypeStruct((1, HD, HD), f32),
        ),
        in_specs=[hbm] * 8,
        out_specs=(vmem, vmem, vmem),
        scratch_shapes=[
            pltpu.SMEM(table.shape, jnp.int32),
            pltpu.SMEM(lengths.shape, jnp.int32),
            pltpu.SMEM((3, 1, NB), f32),
            pltpu.VMEM((ROWS, 3 * HD), bf),
            pltpu.VMEM((POOL, PAGE, 2 * HD), bf),
            pltpu.VMEM((ROWS, 2 * HD), bf),
            pltpu.VMEM((LEAD + ROWS, 2 * HD), bf),
            pltpu.VMEM((ROWS, SPAN), f32),
            pltpu.VMEM((ROWS, SPAN), f32),
            pltpu.VMEM((ROWS, HD), f32),
            pltpu.VMEM((ROWS, 2 * HD), f32),
            pltpu.VMEM((NB, HD + MB, 3 * HD), bf),
            pltpu.VMEM((NB, HD, HD), f32),
            pltpu.VMEM((ROWS, HD), f32),
            pltpu.SemaphoreType.DMA((8 + POOL // CHUNK,)),
        ],
        compiler_params=pltpu.CompilerParams(vmem_limit_bytes=60 << 20),
    )(table, lengths, rates, arrived, persistent, memory, moment, pages)


def columns_kernel(arrived, out, sem):
    copy = pltpu.make_async_copy(arrived.at[:, :, 3 * HD :], out, sem)
    copy.start()
    copy.wait()


def columns_call(arrived):
    members, positions, _ = arrived.shape
    return pl.pallas_call(
        columns_kernel,
        out_shape=jax.ShapeDtypeStruct((members, positions, 2 * HD), bf),
        in_specs=[pl.BlockSpec(memory_space=pltpu.HBM)],
        out_specs=pl.BlockSpec(memory_space=pltpu.HBM),
        scratch_shapes=[pltpu.SemaphoreType.DMA],
        compiler_params=pltpu.CompilerParams(vmem_limit_bytes=60 << 20),
    )(arrived)


def pack_kernel(projected, w_out, packed):
    for request in range(packed.shape[0] // HEADS):
        for head in range(HEADS):
            for part in range(3):
                start = part * D + head * HD
                packed[request * HEADS + head, :, part * HD : (part + 1) * HD] = projected[
                    request, :, start : start + HD
                ]
    weights = jnp.concatenate([w_out[:16, :], w_out[16:, :]], 1)
    for member in range(packed.shape[0]):
        packed[member, :, 3 * HD :] = weights


def pack_call(projected, w_out):
    vmem = pl.BlockSpec(memory_space=pltpu.VMEM)
    groups, positions, _ = projected.shape
    return pl.pallas_call(
        pack_kernel,
        out_shape=jax.ShapeDtypeStruct((groups * HEADS, positions, 5 * HD), bf),
        in_specs=[vmem, vmem],
        out_specs=vmem,
    )(projected, w_out)


def project_kernel(tokens, weights, residual, out):
    groups, _, positions, _ = tokens.shape
    flat = jnp.concatenate(
        [tokens[:, h].reshape(groups * positions, HD) for h in range(HEADS)], 1
    )
    for c in range(weights.shape[0] // 2):
        piece = jnp.concatenate(
            [
                jnp.stack([weights[2 * c + e, :, :, :HD], weights[2 * c + e, :, :, HD:]], 1).reshape(D, HD)
                for e in range(2)
            ],
            1,
        )
        cols = slice(c * 2 * HD, (c + 1) * 2 * HD)
        product = jnp.dot(flat, piece, preferred_element_type=f32)
        here = residual[:, :, cols].astype(f32).reshape(groups * positions, 2 * HD)
        out[:, :, cols] = (here + product).astype(bf).reshape(groups, positions, 2 * HD)


def project_call(tokens, weights, residual):
    vmem = pl.BlockSpec(memory_space=pltpu.VMEM)
    return pl.pallas_call(
        project_kernel,
        out_shape=jax.ShapeDtypeStruct(residual.shape, bf),
        in_specs=[vmem] * 3,
        out_specs=vmem,
        compiler_params=pltpu.CompilerParams(vmem_limit_bytes=32 << 20),
    )(tokens, weights, residual)


def shards(
    projected,
    residual,
    page_store,
    page_table,
    lengths,
    persistent,
    memory_rates,
    memory_state,
    momentum,
    w_out,
):
    groups, positions, _ = projected.shape
    packed = pack_call(projected, w_out)
    arrived = lax.all_to_all(packed, "gy", split_axis=0, concat_axis=0, tiled=True)
    weights = lax.all_gather(columns_call(arrived), "gx", axis=0)
    mixed, memory_next, momentum_next = pair_call(
        page_table,
        lengths,
        memory_rates.transpose(1, 0, 2),
        arrived.reshape(ROWS, 5 * HD),
        persistent,
        memory_state,
        momentum,
        page_store,
    )
    returned = lax.all_to_all(
        mixed.reshape(groups * HEADS, positions, HD), "gy", split_axis=0, concat_axis=0, tiled=True
    )
    layer_out = project_call(
        returned.reshape(groups, HEADS, positions, HD), weights, residual
    )
    return (layer_out, memory_next, momentum_next)


def solution(mesh):
    in_specs = (
        P("gx", "gy", None),
        P("gx", "gy", None),
        P(("gx", "gy"), None, None, None),
        P("gx", None),
        P("gx"),
        P(),
        P(("gx", "gy"), None, None),
        P(("gx", "gy"), None, None),
        P(("gx", "gy"), None, None),
        P("gy", "gx"),
    )
    out_specs = (P("gx", "gy", None), P(("gx", "gy"), None, None), P(("gx", "gy"), None, None))
    return jax.shard_map(shards, mesh=mesh, in_specs=in_specs, out_specs=out_specs, check_vma=False)
```

time: 273 us -> 85.6 us (0.31); the launches traced: 270 us -> 85.3 us
  loops' own time: 127 us -> 0 us
  blocking collectives: 13.9 us -> 48.2 us
  local copies, waits for them, and re-layouts: 32.4 us -> 1.6 us
  matrix products: 30.4 us -> 0 us
  starting transfers between devices: 21.5 us -> 0.04 us
  Pallas kernels: 0 us -> 18.9 us
  other arithmetic: 17.8 us -> 0 us
  between operations: 19.5 us -> 14.1 us
  waiting for transfers between devices: 6.78 us -> 2.56 us
    another operation x1 -> x0, loops' own time: 127 us -> none  [handle(): carried = lax.fori_loop(0, block_count, visit_block, carried)]
    all_to_all x0 -> x2, blocking collectives: none -> 48.2 us  [the longest x1 28.4 us: shards(): lax.all_to_all(packed, 'gy', split_axis=0, concat_axis=0, tiled=True)]
    dot_general x61 -> x0, matrix products: 30.4 us -> none  [the longest x8 12.1 us: recall(): gradient = jnp.dot(key_block.T, errors, precision=lax.Precision.HIGHEST)]
    all_to_all x2 -> x0, starting transfers between devices: 21.5 us -> none  [the longest x1 12 us: shards(): lax.all_to_all(sectioned, 'gy', split_axis=0, concat_axis=1, tiled=True)]
    pallas_call x0 -> x4, Pallas kernels: none -> 18.9 us  [the longest x1 9.05 us: columns_call(): pl.pallas_call(columns_kernel, out_shape=jax.ShapeDtypeStruct((members, p...]
    squeeze x17 -> x0, local copies, waits for them, and re-layouts: 15.4 us -> none  [the longest x16 15.4 us: visit_block(): lax.dynamic_index_in_dim(pages_here, slot_here, 0, keepdims=False)]
    all_gather x1 -> x0, blocking collectives: 13.9 us -> none  [shards(): wide_rows = lax.all_gather(w_out, 'gx', axis=1, tiled=True)]
    dynamic_slice x17 -> x0, local copies, waits for them, and re-layouts: 11.5 us -> none  [the longest x16 10.9 us: visit_block(): lax.dynamic_index_in_dim(table_row, first_page + within_block, 0, keepdim...]
  transfers between devices with their start and end apart: 3 -> 1, of which waited for: 1 -> 1; matrix products, arithmetic and copies ran while one was open for 28% -> 0% of each run, Pallas kernels for 0% -> 8%
where the time goes in v1:
time: 85.6 us; the launch traced here: 85.3 us
  blocking collectives  48.2 us (56%)
  Pallas kernels  18.9 us (22%)
  between operations  14.1 us (16%)
  waiting for transfers between devices  2.56 us (3%)
  local copies, waits for them, and re-layouts  1.6 us (2%)
    all_to_all x1, blocking collectives, shards(): lax.all_to_all(packed, 'gy', split_axis=0, concat_axis=0, tiled=True)  28.4 us
    all_to_all x1, blocking collectives, shards(): lax.all_to_all(mixed.reshape(groups * HEADS, positions, HD), 'gy', split_...  19.9 us
    pallas_call x1, Pallas kernels, columns_call(): pl.pallas_call(columns_kernel, out_shape=jax.ShapeDtypeStruct((members, p...  9.05 us
    pallas_call x1, Pallas kernels, pair_call(): pl.pallas_call(pair_kernel, out_shape=(jax.ShapeDtypeStruct((ROWS, HD), b...  6.74 us
    all_gather x1, waiting for transfers between devices, shards(): weights = lax.all_gather(columns_call(arrived), 'gx', axis=0)  2.55 us
    pallas_call x1, Pallas kernels, pack_call(): pl.pallas_call(pack_kernel, out_shape=jax.ShapeDtypeStruct((groups * HEAD...  1.95 us
  transfers between devices with their start and end apart: 1, of which 1 were waited for; matrix products, arithmetic and copies ran while one was open for 0% of the time, Pallas kernels for 8%

profile of v1, /device:TPU:1, one launch (start us, length us, event | category | flops | bytes accessed | tf_op | source)
XLA Modules:
  0.0 85.3 jit_solution(12041339983986247681)
XLA Ops:
  7.2 0.0 copy-start.1
  7.2 0.0 all-gather.3.cloned.1.call-start
  7.2 2.0 %shard_map.121 = bf16[32,16,640]{2,1,0:T(8,128)(2,1)} custom-call(bf16[4,16,3072]{2,1,0:T(8,128)(2,1)} %projected.1, bf16[32,128]{1,0:T(8,128)(2,1)} %w_out.1), custom_call_target="tpu_custom_call" | custom-call | tf_op jit(solution)/shard_map/pallas_call | solution.py:234
  9.2 28.4 %all_to_all.10.arrived = bf16[32,16,640]{2,1,0:T(8,128)(2,1)} all-to-all(bf16[32,16,640]{2,1,0:T(8,128)(2,1)} %shard_map.121), channel_id=1, replica_groups=mesh['gx'=8,'gy'=32] {'gy'}, dimensions={0} | all-to-all | bytes 1310720 | tf_op jit(solution)/shard_map/all_to_all | solution.py:286
  37.5 9.0 %shard_map.123 = bf16[32,16,256]{2,1,0:T(8,128)(2,1)} custom-call(bf16[32,16,640]{2,1,0:T(8,128)(2,1)} %all_to_all.10.arrived), custom_call_target="tpu_custom_call" | custom-call | tf_op jit(solution)/shard_map/pallas_call | solution.py:208
  46.6 0.0 all-gather.3.cloned.1.call-update
  46.6 6.7 %shard_map.122 = (bf16[512,128]{1,0:T(8,128)(2,1)}, f32[1,128,128]{2,1,0:T(8,128)}, f32[1,128,128]{2,1,0:T(8,128)}) custom-call(s32[4,64]{1,0:T(4,128)} %table_hbm.1, s32[4]{0:T(128)} %lengths_hbm.1, f32[3,1,8]{2,1,0:T(1,128)} %bitcast.9, bf16[512,640]{1,0:T(8,128)(2,1)} %bitcast.7, bf16[2,16,1024]{2,1,0:T(8,128)(2,1)} %persistent.1, ...), custom_call_target="tpu_custom_call" | custom-call | tf_op jit(solution)/shard_map/pallas_call | solution.py:170
  53.4 19.9 %all_to_all.11 = bf16[32,16,128]{2,1,0:T(8,128)(2,1)S(1)} all-to-all(bf16[32,16,128]{2,1,0:T(8,128)(2,1)} %bitcast.8), channel_id=1, replica_groups=mesh['gx'=8,'gy'=32] {'gy'}, dimensions={0} | all-to-all | bytes 262144 | tf_op jit(solution)/shard_map/all_to_all | solution.py:298
  73.2 2.5 %all-gather.3.cloned.1.call-done = bf16[256,16,256]{2,1,0:T(8,128)(2,1)} async-done(((bf16[32,16,256]{2,1,0:T(8,128)(2,1)}), bf16[256,16,256]{2,1,0:T(8,128)(2,1)}) %all-gather.3.cloned.1.call-update) | async-done | bytes 2097168 | tf_op jit(solution)/shard_map/all_gather | solution.py:287
  75.8 0.0 copy-done.1
  75.8 0.0 copy-start
  75.8 1.6 %copy-done = bf16[256,16,256]{2,1,0:T(8,128)(2,1)S(1)} copy-done((bf16[256,16,256]{2,1,0:T(8,128)(2,1)S(1)}, bf16[256,16,256]{2,1,0:T(8,128)(2,1)}, u32[]{:S(2)}) %copy-start) | copy-done | bytes 2097176
  77.4 1.1 %shard_map.124 = bf16[4,16,1024]{2,1,0:T(8,128)(2,1)} custom-call(bf16[4,8,16,128]{3,2,1,0:T(8,128)(2,1)S(1)} %bitcast.6, bf16[8,32,16,256]{3,2,1,0:T(8,128)(2,1)S(1)} %bitcast.5, bf16[4,16,1024]{2,1,0:T(8,128)(2,1)S(1)} %copy-done.1), custom_call_target="tpu_custom_call" | custom-call | tf_op jit(solution)/shard_map/pallas_call | solution.py:263
Async XLA Ops:
  7.2 68.6 %copy-start.1 = (bf16[4,16,1024]{2,1,0:T(8,128)(2,1)S(1)}, bf16[4,16,1024]{2,1,0:T(8,128)(2,1)}, u32[]{:S(2)}) copy-start(bf16[4,16,1024]{2,1,0:T(8,128)(2,1)} %residual.1) | copy-start | bytes 393220
  7.2 68.6 %all-gather.3.cloned.1.call-start = ((), (), s32[]{:S(2)}) async-start(), calls=%async_computation.2 | async-start | bytes 2359296 | tf_op jit(solution)/shard_map/all_gather | solution.py:287
  75.8 1.6 %copy-start = (bf16[256,16,256]{2,1,0:T(8,128)(2,1)S(1)}, bf16[256,16,256]{2,1,0:T(8,128)(2,1)}, u32[]{:S(2)}) copy-start(bf16[256,16,256]{2,1,0:T(8,128)(2,1)} %all-gather.3.cloned.1.call-done) | copy-start | bytes 6291460
Sparse Core Ops, SparseCore 0:
  46.7 28.9 all-gather.2

commit v2 on v1

--- a/solution.py
+++ b/solution.py
@@ -197,24 +197,6 @@
     )(table, lengths, rates, arrived, persistent, memory, moment, pages)
 
 
-def columns_kernel(arrived, out, sem):
-    copy = pltpu.make_async_copy(arrived.at[:, :, 3 * HD :], out, sem)
-    copy.start()
-    copy.wait()
-
-
-def columns_call(arrived):
-    members, positions, _ = arrived.shape
-    return pl.pallas_call(
-        columns_kernel,
-        out_shape=jax.ShapeDtypeStruct((members, positions, 2 * HD), bf),
-        in_specs=[pl.BlockSpec(memory_space=pltpu.HBM)],
-        out_specs=pl.BlockSpec(memory_space=pltpu.HBM),
-        scratch_shapes=[pltpu.SemaphoreType.DMA],
-        compiler_params=pltpu.CompilerParams(vmem_limit_bytes=60 << 20),
-    )(arrived)
-
-
 def pack_kernel(projected, w_out, packed):
     for request in range(packed.shape[0] // HEADS):
         for head in range(HEADS):
@@ -239,34 +221,39 @@
     )(projected, w_out)
 
 
-def project_kernel(tokens, weights, residual, out):
+def project_kernel(tokens, *rest):
+    *blocks, residual, out = rest
+    count = len(blocks) // 2
+    place = lax.axis_index("gx")
+    row, core = place // 2, lax.rem(place, 2)
     groups, _, positions, _ = tokens.shape
     flat = jnp.concatenate(
         [tokens[:, h].reshape(groups * positions, HD) for h in range(HEADS)], 1
     )
-    for c in range(weights.shape[0] // 2):
-        piece = jnp.concatenate(
-            [
-                jnp.stack([weights[2 * c + e, :, :, :HD], weights[2 * c + e, :, :, HD:]], 1).reshape(D, HD)
-                for e in range(2)
-            ],
-            1,
+    for k in range(count):
+        pair = [blocks[k], blocks[count + k]]
+        weights = jnp.concatenate(
+            [jnp.stack([w[:, :, :HD], w[:, :, HD:]], 1).reshape(D, HD) for w in pair], 1
         )
-        cols = slice(c * 2 * HD, (c + 1) * 2 * HD)
-        product = jnp.dot(flat, piece, preferred_element_type=f32)
-        here = residual[:, :, cols].astype(f32).reshape(groups * positions, 2 * HD)
-        out[:, :, cols] = (here + product).astype(bf).reshape(groups, positions, 2 * HD)
-
-
-def project_call(tokens, weights, residual):
+        product = jnp.dot(flat, weights, preferred_element_type=f32)
+        source = lax.rem(row - k + count, count)
+        for e in range(2):
+            start = (2 * source + (core if e == 0 else 1 - core)) * HD
+            cols = pl.ds(pl.multiple_of(start, HD), HD)
+            here = residual[:, :, cols].astype(f32).reshape(groups * positions, HD)
+            total = here + product[:, e * HD : (e + 1) * HD]
+            out[:, :, cols] = total.astype(bf).reshape(groups, positions, HD)
+
+
+def project_call(tokens, blocks, residual):
     vmem = pl.BlockSpec(memory_space=pltpu.VMEM)
     return pl.pallas_call(
         project_kernel,
         out_shape=jax.ShapeDtypeStruct(residual.shape, bf),
-        in_specs=[vmem] * 3,
+        in_specs=[vmem] * (2 + len(blocks)),
         out_specs=vmem,
-        compiler_params=pltpu.CompilerParams(vmem_limit_bytes=32 << 20),
-    )(tokens, weights, residual)
+        compiler_params=pltpu.CompilerParams(vmem_limit_bytes=16 << 20),
+    )(tokens, *blocks, residual)
 
 
 def shards(
@@ -284,7 +271,14 @@
     groups, positions, _ = projected.shape
     packed = pack_call(projected, w_out)
     arrived = lax.all_to_all(packed, "gy", split_axis=0, concat_axis=0, tiled=True)
-    weights = lax.all_gather(columns_call(arrived), "gx", axis=0)
+    own = arrived[:, :, 3 * HD :]
+    chips = lax.axis_size("gx") // 2
+    along = [
+        [(2 * y + c, 2 * ((y + k) % chips) + c) for y in range(chips) for c in range(2)]
+        for k in range(chips)
+    ]
+    across = [(i, i ^ 1) for i in range(2 * chips)]
+    blocks = [own] + [lax.ppermute(own, "gx", along[k]) for k in range(1, chips)]
     mixed, memory_next, momentum_next = pair_call(
         page_table,
         lengths,
@@ -295,11 +289,13 @@
         momentum,
         page_store,
     )
+    mixed, blocks = lax.optimization_barrier((mixed, blocks))
+    others = [lax.ppermute(block, "gx", across) for block in blocks]
     returned = lax.all_to_all(
         mixed.reshape(groups * HEADS, positions, HD), "gy", split_axis=0, concat_axis=0, tiled=True
     )
     layer_out = project_call(
-        returned.reshape(groups, HEADS, positions, HD), weights, residual
+        returned.reshape(groups, HEADS, positions, HD), blocks + others, residual
     )
     return (layer_out, memory_next, momentum_next)
 

time: 85.6 us -> 69.1 us (0.81)
  between operations: 14.1 us -> 0.7 us
  starting transfers between devices: 0.04 us -> 10.2 us
  Pallas kernels: 18.9 us -> 12.2 us
  waiting for transfers between devices: 2.56 us -> 0.02 us
  blocking collectives: 48.2 us -> 45.7 us
  local copies, waits for them, and re-layouts: 1.6 us -> 0.03 us
    ppermute x0 -> x7, starting transfers between devices: none -> 10.2 us  [the longest x4 6.3 us: shards(): others = [lax.ppermute(block, 'gx', across) for block in blocks]]
    pallas_call x1 -> x0, Pallas kernels: 9.05 us -> none  [columns_call(): pl.pallas_call(columns_kernel, out_shape=jax.ShapeDtypeStruct((members, p...]
    all_gather x1 -> x0, waiting for transfers between devices: 2.55 us -> none  [shards(): weights = lax.all_gather(columns_call(arrived), 'gx', axis=0)]
    all_to_all x1, blocking collectives: 19.9 us -> 17.4 us  [shards(): lax.all_to_all(mixed.reshape(groups * HEADS, positions, HD), 'gy', split_...]
    pallas_call x1, Pallas kernels: 6.74 us -> 9.11 us  [pair_call(): pl.pallas_call(pair_kernel, out_shape=(jax.ShapeDtypeStruct((ROWS, HD), b...]
    unnamed x4, local copies, waits for them, and re-layouts: 1.6 us -> 0.01 us
  transfers between devices with their start and end apart: 1 -> 7, of which waited for: 1 -> 0; matrix products, arithmetic and copies ran while one was open for 0% -> 0% of each run, Pallas kernels for 8% -> 13%
where the time goes in v2:
time: 69.1 us; the launch traced here: 68.8 us
  blocking collectives  45.7 us (66%)
  Pallas kernels  12.2 us (18%)
  starting transfers between devices  10.2 us (15%)
  between operations  0.7 us (1%)
    all_to_all x1, blocking collectives, shards(): lax.all_to_all(packed, 'gy', split_axis=0, concat_axis=0, tiled=True)  28.2 us
    all_to_all x1, blocking collectives, shards(): lax.all_to_all(mixed.reshape(groups * HEADS, positions, HD), 'gy', split_...  17.4 us
    pallas_call x1, Pallas kernels, pair_call(): pl.pallas_call(pair_kernel, out_shape=(jax.ShapeDtypeStruct((ROWS, HD), b...  9.11 us
    ppermute x4, starting transfers between devices, shards(): others = [lax.ppermute(block, 'gx', across) for block in blocks]  6.3 us
    ppermute x3, starting transfers between devices, shards(): lax.ppermute(own, 'gx', along[k])  3.85 us
    pallas_call x1, Pallas kernels, pack_call(): pl.pallas_call(pack_kernel, out_shape=jax.ShapeDtypeStruct((groups * HEAD...  1.95 us
  transfers between devices with their start and end apart: 7, of which 0 were waited for; matrix products, arithmetic and copies ran while one was open for 0% of the time, Pallas kernels for 13%

profile of v2, /device:TPU:1, one launch (start us, length us, event | category | flops | bytes accessed | tf_op | source)
XLA Modules:
  0.0 68.8 jit_solution(16480258083195039218)
XLA Ops:
  0.6 0.0 copy-start
  0.6 2.0 %shard_map.121 = bf16[32,16,640]{2,1,0:T(8,128)(2,1)} custom-call(bf16[4,16,3072]{2,1,0:T(8,128)(2,1)} %projected.1, bf16[32,128]{1,0:T(8,128)(2,1)} %w_out.1), custom_call_target="tpu_custom_call" | custom-call | tf_op jit(solution)/shard_map/pallas_call | solution.py:216
  2.6 28.2 %all_to_all.10 = bf16[32,16,640]{2,1,0:T(8,128)(2,1)S(1)} all-to-all(bf16[32,16,640]{2,1,0:T(8,128)(2,1)} %shard_map.121), channel_id=1, replica_groups=mesh['gx'=8,'gy'=32] {'gy'}, dimensions={0} | all-to-all | bytes 1310720 | tf_op jit(solution)/shard_map/all_to_all | solution.py:273
  30.8 0.0 copy-start.1
  30.9 2.8 %collective-permute-start.2 = (bf16[32,16,256]{2,1,0:T(8,128)(2,1)S(1)}, bf16[32,16,256]{2,1,0:T(8,128)(2,1)S(1)}, u32[]{:S(2)}, u32[]{:S(2)}) collective-permute-start(bf16[32,16,256]{2,1,0:T(8,128)(2,1)S(1)} %slice.4.rest_0_), channel_id=1, source_target_pairs={{0,192},{32,224},{64,0},{96,32},{128,64},{160,96},{192,128},{224,1... | collective-permute-start | bytes 786440 | tf_op jit(solution)/shard_map/ppermute | solution.py:281
  33.7 0.3 collective-permute-start.1
  34.0 0.7 %collective-permute-start = (bf16[32,16,256]{2,1,0:T(8,128)(2,1)S(1)}, bf16[32,16,256]{2,1,0:T(8,128)(2,1)S(1)}, u32[]{:S(2)}, u32[]{:S(2)}) collective-permute-start(bf16[32,16,256]{2,1,0:T(8,128)(2,1)S(1)} %slice.4.rest_0_), channel_id=1, source_target_pairs={{0,64},{32,96},{64,128},{96,160},{128,192},{160,224},{192,0},{224,... | collective-permute-start | bytes 786440 | tf_op jit(solution)/shard_map/ppermute | solution.py:281
  34.7 0.0 copy-done.1
  34.7 9.1 %shard_map.122 = (bf16[512,128]{1,0:T(8,128)(2,1)}, f32[1,128,128]{2,1,0:T(8,128)}, f32[1,128,128]{2,1,0:T(8,128)}) custom-call(s32[4,64]{1,0:T(4,128)} %table_hbm.1, s32[4]{0:T(128)} %lengths_hbm.1, f32[3,1,8]{2,1,0:T(1,128)} %bitcast.7, bf16[512,640]{1,0:T(8,128)(2,1)} %bitcast.5, bf16[2,16,1024]{2,1,0:T(8,128)(2,1)} %persistent.1, ...), custom_call_target="tpu_custom_call" | custom-call | tf_op jit(solution)/shard_map/pallas_call | solution.py:170
  43.8 0.0 collective-permute-done.2.rest_3_
  43.8 0.0 collective-permute-done.1.rest_2_
  43.9 0.0 collective-permute-done.rest_1_
  43.9 5.8 %collective-permute-start.3 = (bf16[32,16,256]{2,1,0:T(8,128)(2,1)S(1)}, bf16[32,16,256]{2,1,0:T(8,128)(2,1)S(1)}, u32[]{:S(2)}, u32[]{:S(2)}) collective-permute-start(bf16[32,16,256]{2,1,0:T(8,128)(2,1)S(1)} %slice.4.rest_0_), channel_id=1, source_target_pairs={{0,32},{32,0},{64,96},{96,64},{128,160},{160,128},{192,224},{224,1... | collective-permute-start | bytes 786440 | tf_op jit(solution)/shard_map/ppermute | solution.py:293
  49.7 0.0 collective-permute-start.4
  49.7 0.5 collective-permute-start.5
  50.2 0.0 collective-permute-start.6
  50.2 17.4 %all_to_all.11 = bf16[32,16,128]{2,1,0:T(8,128)(2,1)S(1)} all-to-all(bf16[32,16,128]{2,1,0:T(8,128)(2,1)} %bitcast.6), channel_id=1, replica_groups=mesh['gx'=8,'gy'=32] {'gy'}, dimensions={0} | all-to-all | bytes 262144 | tf_op jit(solution)/shard_map/all_to_all | solution.py:294
  67.6 0.0 collective-permute-done.3.rest_4_
  67.6 0.0 collective-permute-done.4.rest_5_
  67.6 0.0 collective-permute-done.5.rest_6_
  67.6 0.0 collective-permute-done.6.rest_7_
  67.6 0.0 copy-done
  67.6 1.1 %shard_map.123 = bf16[4,16,1024]{2,1,0:T(8,128)(2,1)} custom-call(bf16[4,8,16,128]{3,2,1,0:T(8,128)(2,1)S(1)} %bitcast.4, bf16[32,16,256]{2,1,0:T(8,128)(2,1)S(1)} %slice.4.rest_0_, bf16[32,16,256]{2,1,0:T(8,128)(2,1)S(1)} %collective-permute-done.rest_1_, bf16[32,16,256]{2,1,0:T(8,128)(2,1)S(1)} %collective-permute-done.1.rest_2_, ...), custom_call_target="tpu_custom_call" | custom-call | tf_op jit(solution)/shard_map/pallas_call | solution.py:250
  (1 shorter events, 0.0 us)
Async XLA Ops:
  0.6 67.0 %copy-start = (bf16[4,16,1024]{2,1,0:T(8,128)(2,1)S(1)}, bf16[4,16,1024]{2,1,0:T(8,128)(2,1)}, u32[]{:S(2)}) copy-start(bf16[4,16,1024]{2,1,0:T(8,128)(2,1)} %rest_8_.1) | copy-start | bytes 393220
  30.8 3.9 %copy-start.1 = (bf16[32,16,640]{2,1,0:T(8,128)(2,1)}, bf16[32,16,640]{2,1,0:T(8,128)(2,1)S(1)}, u32[]{:S(2)}) copy-start(bf16[32,16,640]{2,1,0:T(8,128)(2,1)S(1)} %all_to_all.10) | copy-start | bytes 1966084
  30.9 13.0 %collective-permute-start.2 = (bf16[32,16,256]{2,1,0:T(8,128)(2,1)S(1)}, bf16[32,16,256]{2,1,0:T(8,128)(2,1)S(1)}, u32[]{:S(2)}, u32[]{:S(2)}) collective-permute-start(bf16[32,16,256]{2,1,0:T(8,128)(2,1)S(1)} %slice.4.rest_0_), channel_id=1, source_target_pairs={{0,192},{32,224},{64,0},{96,32},{128,64},{160,96},{192,128},{224,1... | collective-permute-start | bytes 786440 | tf_op jit(solution)/shard_map/ppermute | solution.py:281
  33.7 10.2 %collective-permute-start.1 = (bf16[32,16,256]{2,1,0:T(8,128)(2,1)S(1)}, bf16[32,16,256]{2,1,0:T(8,128)(2,1)S(1)}, u32[]{:S(2)}, u32[]{:S(2)}) collective-permute-start(bf16[32,16,256]{2,1,0:T(8,128)(2,1)S(1)} %slice.4.rest_0_), channel_id=1, source_target_pairs={{0,128},{32,160},{64,192},{96,224},{128,0},{160,32},{192,64},{224,... | collective-permute-start | bytes 786440 | tf_op jit(solution)/shard_map/ppermute | solution.py:281
  34.0 9.8 %collective-permute-start = (bf16[32,16,256]{2,1,0:T(8,128)(2,1)S(1)}, bf16[32,16,256]{2,1,0:T(8,128)(2,1)S(1)}, u32[]{:S(2)}, u32[]{:S(2)}) collective-permute-start(bf16[32,16,256]{2,1,0:T(8,128)(2,1)S(1)} %slice.4.rest_0_), channel_id=1, source_target_pairs={{0,64},{32,96},{64,128},{96,160},{128,192},{160,224},{192,0},{224,... | collective-permute-start | bytes 786440 | tf_op jit(solution)/shard_map/ppermute | solution.py:281
  43.9 23.7 %collective-permute-start.3 = (bf16[32,16,256]{2,1,0:T(8,128)(2,1)S(1)}, bf16[32,16,256]{2,1,0:T(8,128)(2,1)S(1)}, u32[]{:S(2)}, u32[]{:S(2)}) collective-permute-start(bf16[32,16,256]{2,1,0:T(8,128)(2,1)S(1)} %slice.4.rest_0_), channel_id=1, source_target_pairs={{0,32},{32,0},{64,96},{96,64},{128,160},{160,128},{192,224},{224,1... | collective-permute-start | bytes 786440 | tf_op jit(solution)/shard_map/ppermute | solution.py:293
  49.7 18.0 %collective-permute-start.4 = (bf16[32,16,256]{2,1,0:T(8,128)(2,1)S(1)}, bf16[32,16,256]{2,1,0:T(8,128)(2,1)S(1)}, u32[]{:S(2)}, u32[]{:S(2)}) collective-permute-start(bf16[32,16,256]{2,1,0:T(8,128)(2,1)S(1)} %collective-permute-done.rest_1_), channel_id=1, source_target_pairs={{0,32},{32,0},{64,96},{96,64},{128,160},{160,128},{192,224},{224,1... | collective-permute-start | bytes 786440 | tf_op jit(solution)/shard_map/ppermute | solution.py:293
  49.7 18.0 %collective-permute-start.5 = (bf16[32,16,256]{2,1,0:T(8,128)(2,1)S(1)}, bf16[32,16,256]{2,1,0:T(8,128)(2,1)S(1)}, u32[]{:S(2)}, u32[]{:S(2)}) collective-permute-start(bf16[32,16,256]{2,1,0:T(8,128)(2,1)S(1)} %collective-permute-done.1.rest_2_), channel_id=1, source_target_pairs={{0,32},{32,0},{64,96},{96,64},{128,160},{160,128},{192,224},{224,1... | collective-permute-start | bytes 786440 | tf_op jit(solution)/shard_map/ppermute | solution.py:293
  50.2 17.5 %collective-permute-start.6 = (bf16[32,16,256]{2,1,0:T(8,128)(2,1)S(1)}, bf16[32,16,256]{2,1,0:T(8,128)(2,1)S(1)}, u32[]{:S(2)}, u32[]{:S(2)}) collective-permute-start(bf16[32,16,256]{2,1,0:T(8,128)(2,1)S(1)} %collective-permute-done.2.rest_3_), channel_id=1, source_target_pairs={{0,32},{32,0},{64,96},{96,64},{128,160},{160,128},{192,224},{224,1... | collective-permute-start | bytes 786440 | tf_op jit(solution)/shard_map/ppermute | solution.py:293

commit v3 on v2

--- a/solution.py
+++ b/solution.py
@@ -13,7 +13,6 @@
 PPB = SPAN // PAGE
 BLOCKS = MAXP // PPB
 LEAD = 128
-POOL, CHUNK = 72, 9
 SCALE = HD ** (-0.5) * math.log2(math.e)
 LOW = -1e30
 bf, f32 = jnp.bfloat16, jnp.float32
@@ -49,21 +48,29 @@
     request, head = member // HEADS, lax.rem(member, HEADS)
     columns = pl.ds(pl.multiple_of(head * HD, HD), HD)
     moves = [
+        (table_hbm, table),
         (arrived.at[:, : 3 * HD], qkv),
         (persistent.at[0, :, columns], lead.at[:PERSIST, :HD]),
         (persistent.at[1, :, columns], lead.at[:PERSIST, HD:]),
-        (table_hbm, table),
         (lengths_hbm, lengths),
         (rates_hbm, rates),
         (memory_in, memory_out),
         (moment_in, moment_out),
-    ] + [
-        (pages_hbm.at[0, pl.ds(i, CHUNK)], pages.at[pl.ds(i, CHUNK)]) for i in range(0, POOL, CHUNK)
     ]
     copies = [pltpu.make_async_copy(a, b, sems.at[i]) for i, (a, b) in enumerate(moves)]
     for copy in copies:
         copy.start()
     copies[0].wait()
+    for i in range(MAXP):
+        pltpu.make_async_copy(
+            pages_hbm.at[0, table[request, i]], pages.at[i], sems.at[8 + i // PPB]
+        ).start()
+
+    def arrive(b):
+        part = pages.at[pl.ds(b * PPB, PPB)]
+        pltpu.make_async_copy(part, part, sems.at[8 + b]).wait()
+
+    copies[1].wait()
 
     queries = qkv[:, :HD].astype(f32)
     high, low = halves(queries * SCALE)
@@ -100,8 +107,8 @@
         moment_out[0] = moment
         memory_out[0] = (1.0 - rates[2, 0, b]) * memory + moment
 
-    copies[1].wait()
     copies[2].wait()
+    copies[3].wait()
     lead[PERSIST:LEAD, :] = jnp.zeros((LEAD - PERSIST, 2 * HD), bf)
     lead[LEAD:, :] = qkv[:, HD : 3 * HD]
     width = LEAD + ROWS
@@ -117,14 +124,14 @@
     sums[...] = jnp.dot(
         weights.astype(bf), jnp.concatenate([lead[:, HD:], ones], 1), preferred_element_type=f32
     )
-    for copy in copies[3:]:
+    for copy in copies[4:]:
         copy.wait()
+    arrive(0)
     length = lengths[request]
 
     def page_of(b, columns):
-        return jnp.concatenate(
-            [pages[table[request, jnp.minimum(b * PPB + i, MAXP - 1)], :, columns] for i in range(PPB)], 0
-        )
+        start = jnp.minimum(b * PPB, MAXP - PPB)
+        return pages[pl.ds(start, PPB), :, columns].reshape(SPAN, HD)
 
     def score(b, scores):
         keys = page_of(b, slice(0, HD))
@@ -146,6 +153,12 @@
     twos = (length + 2 * SPAN - 1) // (2 * SPAN)
 
     def two_blocks(i, carry):
+        arrive(2 * i + 1)
+
+        @pl.when(2 * i + 2 < BLOCKS)
+        def _():
+            arrive(2 * i + 2)
+
         score(2 * i + 1, scores_b)
         absorb(2 * i, scores_a)
         memory_step(2 * i)
@@ -157,6 +170,10 @@
     lax.fori_loop(0, twos, two_blocks, 0)
 
     def rest(b, carry):
+        @pl.when(b > 2 * twos)
+        def _():
+            arrive(b)
+
         memory_step(b)
         return carry
 
@@ -181,7 +198,7 @@
             pltpu.SMEM(lengths.shape, jnp.int32),
             pltpu.SMEM((3, 1, NB), f32),
             pltpu.VMEM((ROWS, 3 * HD), bf),
-            pltpu.VMEM((POOL, PAGE, 2 * HD), bf),
+            pltpu.VMEM((MAXP, PAGE, 2 * HD), bf),
             pltpu.VMEM((ROWS, 2 * HD), bf),
             pltpu.VMEM((LEAD + ROWS, 2 * HD), bf),
             pltpu.VMEM((ROWS, SPAN), f32),
@@ -191,7 +208,7 @@
             pltpu.VMEM((NB, HD + MB, 3 * HD), bf),
             pltpu.VMEM((NB, HD, HD), f32),
             pltpu.VMEM((ROWS, HD), f32),
-            pltpu.SemaphoreType.DMA((8 + POOL // CHUNK,)),
+            pltpu.SemaphoreType.DMA((8 + BLOCKS,)),
         ],
         compiler_params=pltpu.CompilerParams(vmem_limit_bytes=60 << 20),
     )(table, lengths, rates, arrived, persistent, memory, moment, pages)
@@ -254,6 +271,22 @@
         out_specs=vmem,
         compiler_params=pltpu.CompilerParams(vmem_limit_bytes=16 << 20),
     )(tokens, *blocks, residual)
+
+
+def hold_kernel(*refs):
+    pass
+
+
+def hold_call(blocks, *after):
+    return pl.pallas_call(
+        hold_kernel,
+        out_shape=[jax.ShapeDtypeStruct(block.shape, block.dtype) for block in blocks],
+        in_specs=[pl.BlockSpec(memory_space=pl.ANY)] * (len(blocks) + len(after)),
+        out_specs=[pl.BlockSpec(memory_space=pl.ANY)] * len(blocks),
+        input_output_aliases={i: i for i in range(len(blocks))},
+        compiler_params=pltpu.CompilerParams(vmem_limit_bytes=16 << 20),
+        cost_estimate=pl.CostEstimate(flops=0, bytes_accessed=0, transcendentals=0),
+    )(*blocks, *after)
 
 
 def shards(
@@ -278,7 +311,8 @@
         for k in range(chips)
     ]
     across = [(i, i ^ 1) for i in range(2 * chips)]
-    blocks = [own] + [lax.ppermute(own, "gx", along[k]) for k in range(1, chips)]
+    below, above = [lax.ppermute(own, "gx", along[k]) for k in (1, chips - 1)]
+    beside = lax.ppermute(own, "gx", across)
     mixed, memory_next, momentum_next = pair_call(
         page_table,
         lengths,
@@ -289,11 +323,15 @@
         momentum,
         page_store,
     )
-    mixed, blocks = lax.optimization_barrier((mixed, blocks))
-    others = [lax.ppermute(block, "gx", across) for block in blocks]
     returned = lax.all_to_all(
         mixed.reshape(groups * HEADS, positions, HD), "gy", split_axis=0, concat_axis=0, tiled=True
     )
+    below, above, memory_next = hold_call([below, above, memory_next])
+    far = lax.ppermute(below, "gx", along[1])
+    near = [lax.ppermute(block, "gx", across) for block in (below, above)]
+    returned, far = lax.optimization_barrier((returned, far))
+    blocks = [own, below, far, above]
+    others = [beside, near[0], lax.ppermute(far, "gx", across), near[1]]
     layer_out = project_call(
         returned.reshape(groups, HEADS, positions, HD), blocks + others, residual
     )

time: 69.1 us -> 67.7 us (0.980)
  blocking collectives: 45.7 us -> 28.2 us
  starting transfers between devices: 10.2 us -> 21.3 us
  waiting for transfers between devices: 0.02 us -> 7.44 us
  Pallas kernels: 12.2 us -> 9.83 us
    all_to_all x1 -> x0, blocking collectives: 17.4 us -> none  [shards(): lax.all_to_all(mixed.reshape(groups * HEADS, positions, HD), 'gy', split_...]
    all_to_all x0 -> x1, starting transfers between devices: none -> 12 us  [shards(): lax.all_to_all(mixed.reshape(groups * HEADS, positions, HD), 'gy', split_...]
    all_to_all x0 -> x1, waiting for transfers between devices: none -> 6.27 us  [shards(): lax.all_to_all(mixed.reshape(groups * HEADS, positions, HD), 'gy', split_...]
    pallas_call x1, Pallas kernels: 9.11 us -> 6.72 us  [pair_call(): pl.pallas_call(pair_kernel, out_shape=(jax.ShapeDtypeStruct((ROWS, HD), b...]
    ppermute x7, waiting for transfers between devices: 0.02 us -> 1.17 us  [the longest x1 1.15 us: shards(): others = [beside, near[0], lax.ppermute(far, 'gx', across), near[1]]]
    ppermute x7, starting transfers between devices: 10.2 us -> 9.35 us  [the longest x1 3.54 us: shards(): others = [beside, near[0], lax.ppermute(far, 'gx', across), near[1]]]
  transfers between devices with their start and end apart: 7 -> 8, of which waited for: 0 -> 2; matrix products, arithmetic and copies ran while one was open for 0% -> 0% of each run, Pallas kernels for 13% -> 10%
where the time goes in v3:
time: 67.7 us; the launch traced here: 67.6 us
  blocking collectives  28.2 us (42%)
  starting transfers between devices  21.3 us (31%)
  Pallas kernels  9.83 us (15%)
  waiting for transfers between devices  7.44 us (11%)
  between operations  0.69 us (1%)
    all_to_all x1, blocking collectives, shards(): lax.all_to_all(packed, 'gy', split_axis=0, concat_axis=0, tiled=True)  28.2 us
    all_to_all x1, starting transfers between devices, shards(): lax.all_to_all(mixed.reshape(groups * HEADS, positions, HD), 'gy', split_...  12 us
    pallas_call x1, Pallas kernels, pair_call(): pl.pallas_call(pair_kernel, out_shape=(jax.ShapeDtypeStruct((ROWS, HD), b...  6.72 us
    all_to_all x1, waiting for transfers between devices, shards(): lax.all_to_all(mixed.reshape(groups * HEADS, positions, HD), 'gy', split_...  6.27 us
    ppermute x1, starting transfers between devices, shards(): others = [beside, near[0], lax.ppermute(far, 'gx', across), near[1]]  3.54 us
    ppermute x2, starting transfers between devices, shards(): below, above = [lax.ppermute(own, 'gx', along[k]) for k in (1, chips - 1)]  2.81 us
    ppermute x1, starting transfers between devices, shards(): beside = lax.ppermute(own, 'gx', across)  2.39 us
    pallas_call x1, Pallas kernels, pack_call(): pl.pallas_call(pack_kernel, out_shape=jax.ShapeDtypeStruct((groups * HEAD...  1.96 us
  transfers between devices with their start and end apart: 8, of which 2 were waited for; matrix products, arithmetic and copies ran while one was open for 0% of the time, Pallas kernels for 10%

profile of v3, /device:TPU:1, one launch (start us, length us, event | category | flops | bytes accessed | tf_op | source)
XLA Modules:
  0.0 67.6 jit_solution(16489266022353798801)
XLA Ops:
  0.6 0.0 copy-start
  0.6 2.0 %shard_map.121 = bf16[32,16,640]{2,1,0:T(8,128)(2,1)} custom-call(bf16[4,16,3072]{2,1,0:T(8,128)(2,1)} %projected.1, bf16[32,128]{1,0:T(8,128)(2,1)} %w_out.1), custom_call_target="tpu_custom_call" | custom-call | tf_op jit(solution)/shard_map/pallas_call | solution.py:233
  2.6 28.2 %all_to_all.10 = bf16[32,16,640]{2,1,0:T(8,128)(2,1)S(1)} all-to-all(bf16[32,16,640]{2,1,0:T(8,128)(2,1)} %shard_map.121), channel_id=1, replica_groups=mesh['gx'=8,'gy'=32] {'gy'}, dimensions={0} | all-to-all | bytes 1310720 | tf_op jit(solution)/shard_map/all_to_all | solution.py:306
  30.8 0.0 copy-start.1
  30.9 2.8 %collective-permute-start.1 = (bf16[32,16,256]{2,1,0:T(8,128)(2,1)S(1)}, bf16[32,16,256]{2,1,0:T(8,128)(2,1)S(1)}, u32[]{:S(2)}, u32[]{:S(2)}) collective-permute-start(bf16[32,16,256]{2,1,0:T(8,128)(2,1)S(1)} %slice.4.rest_0_), channel_id=1, source_target_pairs={{0,192},{32,224},{64,0},{96,32},{128,64},{160,96},{192,128},{224,1... | collective-permute-start | bytes 786440 | tf_op jit(solution)/shard_map/ppermute | solution.py:314
  33.7 0.0 collective-permute-start
  33.7 0.0 copy-done.1
  33.7 6.7 %shard_map.122 = (bf16[512,128]{1,0:T(8,128)(2,1)}, f32[1,128,128]{2,1,0:T(8,128)}, f32[1,128,128]{2,1,0:T(8,128)}) custom-call(s32[4,64]{1,0:T(4,128)} %table_hbm.1, s32[4]{0:T(128)} %lengths_hbm.1, f32[3,1,8]{2,1,0:T(1,128)} %bitcast.7, bf16[512,640]{1,0:T(8,128)(2,1)} %bitcast.5, bf16[2,16,1024]{2,1,0:T(8,128)(2,1)} %persistent.1, ...), custom_call_target="tpu_custom_call" | custom-call | tf_op jit(solution)/shard_map/pallas_call | solution.py:187
  40.4 0.0 collective-permute-done.1.refs_1_
  40.4 0.0 collective-permute-done.refs_0_
  40.4 0.1 collective-permute-start.2
  40.5 12.0 %all-to-all-start.1 = ((bf16[32,16,128]{2,1,0:T(8,128)(2,1)}), bf16[32,16,128]{2,1,0:T(8,128)(2,1)S(1)}, u32[]{:S(2)}, u32[]{:S(2)}) async-start(bf16[32,16,128]{2,1,0:T(8,128)(2,1)} %bitcast.6), calls=%async_computation.1 | async-start | bytes 262144 | tf_op jit(solution)/shard_map/all_to_all | solution.py:326
  52.5 2.4 %collective-permute-start.3 = (bf16[32,16,256]{2,1,0:T(8,128)(2,1)S(1)}, bf16[32,16,256]{2,1,0:T(8,128)(2,1)S(1)}, u32[]{:S(2)}, u32[]{:S(2)}) collective-permute-start(bf16[32,16,256]{2,1,0:T(8,128)(2,1)S(1)} %slice.4.rest_0_), channel_id=1, source_target_pairs={{0,32},{32,0},{64,96},{96,64},{128,160},{160,128},{192,224},{224,1... | collective-permute-start | bytes 786440 | tf_op jit(solution)/shard_map/ppermute | solution.py:315
  54.9 0.1 collective-permute-start.4
  55.0 0.4 collective-permute-start.6
  55.4 6.3 %all-to-all-done.1 = bf16[32,16,128]{2,1,0:T(8,128)(2,1)S(1)} async-done(((bf16[32,16,128]{2,1,0:T(8,128)(2,1)}), bf16[32,16,128]{2,1,0:T(8,128)(2,1)S(1)}, u32[]{:S(2)}, u32[]{:S(2)}) %all-to-all-start.1) | async-done | bytes 131104 | tf_op jit(solution)/shard_map/all_to_all | solution.py:326
  61.7 0.0 collective-permute-done.2.rest_2_
  61.7 3.5 %collective-permute-start.5 = (bf16[32,16,256]{2,1,0:T(8,128)(2,1)S(1)}, bf16[32,16,256]{2,1,0:T(8,128)(2,1)S(1)}, u32[]{:S(2)}, u32[]{:S(2)}) collective-permute-start(bf16[32,16,256]{2,1,0:T(8,128)(2,1)S(1)} %collective-permute-done.2.rest_2_), channel_id=1, source_target_pairs={{0,32},{32,0},{64,96},{96,64},{128,160},{160,128},{192,224},{224,1... | collective-permute-start | bytes 786440 | tf_op jit(solution)/shard_map/ppermute | solution.py:334
  65.2 0.0 collective-permute-done.3.rest_4_
  65.2 0.0 collective-permute-done.6.rest_7_
  65.3 0.0 collective-permute-done.4.rest_5_
  65.3 1.1 %collective-permute-done.5.rest_6_ = bf16[32,16,256]{2,1,0:T(8,128)(2,1)S(1)} collective-permute-done((bf16[32,16,256]{2,1,0:T(8,128)(2,1)S(1)}, bf16[32,16,256]{2,1,0:T(8,128)(2,1)S(1)}, u32[]{:S(2)}, u32[]{:S(2)}) %collective-permute-start.5) | collective-permute-done | bytes 262176 | tf_op jit(solution)/shard_map/ppermute | solution.py:334
  66.4 0.0 copy-done
  66.4 1.1 %shard_map.124 = bf16[4,16,1024]{2,1,0:T(8,128)(2,1)} custom-call(bf16[4,8,16,128]{3,2,1,0:T(8,128)(2,1)S(1)} %bitcast.4, bf16[32,16,256]{2,1,0:T(8,128)(2,1)S(1)} %slice.4.rest_0_, bf16[32,16,256]{2,1,0:T(8,128)(2,1)S(1)} %get-tuple-element.13.rest_1_, bf16[32,16,256]{2,1,0:T(8,128)(2,1)S(1)} %collective-permute-done.2.rest_2_, ...), custom_call_target="tpu_custom_call" | custom-call | tf_op jit(solution)/shard_map/pallas_call | solution.py:267
  (2 shorter events, 0.0 us)
Async XLA Ops:
  0.6 65.8 %copy-start = (bf16[4,16,1024]{2,1,0:T(8,128)(2,1)S(1)}, bf16[4,16,1024]{2,1,0:T(8,128)(2,1)}, u32[]{:S(2)}) copy-start(bf16[4,16,1024]{2,1,0:T(8,128)(2,1)} %rest_8_.1) | copy-start | bytes 393220
  30.8 2.8 %copy-start.1 = (bf16[32,16,640]{2,1,0:T(8,128)(2,1)}, bf16[32,16,640]{2,1,0:T(8,128)(2,1)S(1)}, u32[]{:S(2)}) copy-start(bf16[32,16,640]{2,1,0:T(8,128)(2,1)S(1)} %all_to_all.10) | copy-start | bytes 1966084
  30.9 9.5 %collective-permute-start.1 = (bf16[32,16,256]{2,1,0:T(8,128)(2,1)S(1)}, bf16[32,16,256]{2,1,0:T(8,128)(2,1)S(1)}, u32[]{:S(2)}, u32[]{:S(2)}) collective-permute-start(bf16[32,16,256]{2,1,0:T(8,128)(2,1)S(1)} %slice.4.rest_0_), channel_id=1, source_target_pairs={{0,192},{32,224},{64,0},{96,32},{128,64},{160,96},{192,128},{224,1... | collective-permute-start | bytes 786440 | tf_op jit(solution)/shard_map/ppermute | solution.py:314
  33.7 6.7 %collective-permute-start = (bf16[32,16,256]{2,1,0:T(8,128)(2,1)S(1)}, bf16[32,16,256]{2,1,0:T(8,128)(2,1)S(1)}, u32[]{:S(2)}, u32[]{:S(2)}) collective-permute-start(bf16[32,16,256]{2,1,0:T(8,128)(2,1)S(1)} %slice.4.rest_0_), channel_id=1, source_target_pairs={{0,64},{32,96},{64,128},{96,160},{128,192},{160,224},{192,0},{224,... | collective-permute-start | bytes 786440 | tf_op jit(solution)/shard_map/ppermute | solution.py:314
  40.4 21.3 %collective-permute-start.2 = (bf16[32,16,256]{2,1,0:T(8,128)(2,1)S(1)}, bf16[32,16,256]{2,1,0:T(8,128)(2,1)S(1)}, u32[]{:S(2)}, u32[]{:S(2)}) collective-permute-start(bf16[32,16,256]{2,1,0:T(8,128)(2,1)S(1)} %get-tuple-element.13.rest_1_), channel_id=1, source_target_pairs={{0,64},{32,96},{64,128},{96,160},{128,192},{160,224},{192,0},{224,... | collective-permute-start | bytes 786440 | tf_op jit(solution)/shard_map/ppermute | solution.py:330
  40.5 21.2 %all-to-all-start.1 = ((bf16[32,16,128]{2,1,0:T(8,128)(2,1)}), bf16[32,16,128]{2,1,0:T(8,128)(2,1)S(1)}, u32[]{:S(2)}, u32[]{:S(2)}) async-start(bf16[32,16,128]{2,1,0:T(8,128)(2,1)} %bitcast.6), calls=%async_computation.1 | async-start | bytes 262144 | tf_op jit(solution)/shard_map/all_to_all | solution.py:326
  52.5 12.7 %collective-permute-start.3 = (bf16[32,16,256]{2,1,0:T(8,128)(2,1)S(1)}, bf16[32,16,256]{2,1,0:T(8,128)(2,1)S(1)}, u32[]{:S(2)}, u32[]{:S(2)}) collective-permute-start(bf16[32,16,256]{2,1,0:T(8,128)(2,1)S(1)} %slice.4.rest_0_), channel_id=1, source_target_pairs={{0,32},{32,0},{64,96},{96,64},{128,160},{160,128},{192,224},{224,1... | collective-permute-start | bytes 786440 | tf_op jit(solution)/shard_map/ppermute | solution.py:315
  54.9 10.3 %collective-permute-start.4 = (bf16[32,16,256]{2,1,0:T(8,128)(2,1)S(1)}, bf16[32,16,256]{2,1,0:T(8,128)(2,1)S(1)}, u32[]{:S(2)}, u32[]{:S(2)}) collective-permute-start(bf16[32,16,256]{2,1,0:T(8,128)(2,1)S(1)} %get-tuple-element.13.rest_1_), channel_id=1, source_target_pairs={{0,32},{32,0},{64,96},{96,64},{128,160},{160,128},{192,224},{224,1... | collective-permute-start | bytes 786440 | tf_op jit(solution)/shard_map/ppermute | solution.py:331
  55.0 10.2 %collective-permute-start.6 = (bf16[32,16,256]{2,1,0:T(8,128)(2,1)S(1)}, bf16[32,16,256]{2,1,0:T(8,128)(2,1)S(1)}, u32[]{:S(2)}, u32[]{:S(2)}) collective-permute-start(bf16[32,16,256]{2,1,0:T(8,128)(2,1)S(1)} %get-tuple-element.16.rest_3_), channel_id=1, source_target_pairs={{0,32},{32,0},{64,96},{96,64},{128,160},{160,128},{192,224},{224,1... | collective-permute-start | bytes 786440 | tf_op jit(solution)/shard_map/ppermute | solution.py:331
  61.7 4.7 %collective-permute-start.5 = (bf16[32,16,256]{2,1,0:T(8,128)(2,1)S(1)}, bf16[32,16,256]{2,1,0:T(8,128)(2,1)S(1)}, u32[]{:S(2)}, u32[]{:S(2)}) collective-permute-start(bf16[32,16,256]{2,1,0:T(8,128)(2,1)S(1)} %collective-permute-done.2.rest_2_), channel_id=1, source_target_pairs={{0,32},{32,0},{64,96},{96,64},{128,160},{160,128},{192,224},{224,1... | collective-permute-start | bytes 786440 | tf_op jit(solution)/shard_map/ppermute | solution.py:334

commit v4 on v3

--- a/solution.py
+++ b/solution.py
@@ -49,28 +49,31 @@
     columns = pl.ds(pl.multiple_of(head * HD, HD), HD)
     moves = [
         (table_hbm, table),
-        (arrived.at[:, : 3 * HD], qkv),
+        (arrived.at[pl.ds(0, 128), : 3 * HD], qkv.at[pl.ds(0, 128)]),
         (persistent.at[0, :, columns], lead.at[:PERSIST, :HD]),
         (persistent.at[1, :, columns], lead.at[:PERSIST, HD:]),
         (lengths_hbm, lengths),
         (rates_hbm, rates),
         (memory_in, memory_out),
         (moment_in, moment_out),
+    ] + [
+        (arrived.at[pl.ds(i, 128), : 3 * HD], qkv.at[pl.ds(i, 128)]) for i in range(128, ROWS, 128)
     ]
     copies = [pltpu.make_async_copy(a, b, sems.at[i]) for i, (a, b) in enumerate(moves)]
-    for copy in copies:
+    for copy in copies[:2] + copies[8:] + copies[2:8]:
         copy.start()
     copies[0].wait()
     for i in range(MAXP):
         pltpu.make_async_copy(
-            pages_hbm.at[0, table[request, i]], pages.at[i], sems.at[8 + i // PPB]
+            pages_hbm.at[0, table[request, i]], pages.at[i], sems.at[11 + i // PPB]
         ).start()
 
     def arrive(b):
         part = pages.at[pl.ds(b * PPB, PPB)]
-        pltpu.make_async_copy(part, part, sems.at[8 + b]).wait()
-
-    copies[1].wait()
+        pltpu.make_async_copy(part, part, sems.at[11 + b]).wait()
+
+    for copy in copies[1:2] + copies[8:]:
+        copy.wait()
 
     queries = qkv[:, :HD].astype(f32)
     high, low = halves(queries * SCALE)
@@ -124,7 +127,7 @@
     sums[...] = jnp.dot(
         weights.astype(bf), jnp.concatenate([lead[:, HD:], ones], 1), preferred_element_type=f32
     )
-    for copy in copies[4:]:
+    for copy in copies[4:8]:
         copy.wait()
     arrive(0)
     length = lengths[request]
@@ -208,7 +211,7 @@
             pltpu.VMEM((NB, HD + MB, 3 * HD), bf),
             pltpu.VMEM((NB, HD, HD), f32),
             pltpu.VMEM((ROWS, HD), f32),
-            pltpu.SemaphoreType.DMA((8 + BLOCKS,)),
+            pltpu.SemaphoreType.DMA((11 + BLOCKS,)),
         ],
         compiler_params=pltpu.CompilerParams(vmem_limit_bytes=60 << 20),
     )(table, lengths, rates, arrived, persistent, memory, moment, pages)
@@ -328,10 +331,10 @@
     )
     below, above, memory_next = hold_call([below, above, memory_next])
     far = lax.ppermute(below, "gx", along[1])
+    diagonal = lax.ppermute(below, "gx", [(i, j ^ 1) for i, j in along[1]])
     near = [lax.ppermute(block, "gx", across) for block in (below, above)]
-    returned, far = lax.optimization_barrier((returned, far))
     blocks = [own, below, far, above]
-    others = [beside, near[0], lax.ppermute(far, "gx", across), near[1]]
+    others = [beside, near[0], diagonal, near[1]]
     layer_out = project_call(
         returned.reshape(groups, HEADS, positions, HD), blocks + others, residual
     )

time: 67.7 us -> 67.8 us (level)
  the two profiles are of different devices: /device:TPU:1 before, /device:TPU:8 now
where the time goes in v4:
time: 67.8 us; the launch traced here: 67.1 us
  blocking collectives  49.6 us (73%)
  Pallas kernels  13.5 us (20%)
  starting transfers between devices  3.29 us (5%)
  between operations  0.72 us (1%)
    all_to_all x1, blocking collectives, shards(): lax.all_to_all(packed, 'gy', split_axis=0, concat_axis=0, tiled=True)  31.8 us
    all_to_all x1, blocking collectives, shards(): lax.all_to_all(mixed.reshape(groups * HEADS, positions, HD), 'gy', split_...  17.8 us
    pallas_call x1, Pallas kernels, pair_call(): pl.pallas_call(pair_kernel, out_shape=(jax.ShapeDtypeStruct((ROWS, HD), b...  10.4 us
    ppermute x2, starting transfers between devices, shards(): below, above = [lax.ppermute(own, 'gx', along[k]) for k in (1, chips - 1)]  2.1 us
    pallas_call x1, Pallas kernels, pack_call(): pl.pallas_call(pack_kernel, out_shape=jax.ShapeDtypeStruct((groups * HEAD...  1.97 us
  transfers between devices with their start and end apart: 7, of which 0 were waited for; matrix products, arithmetic and copies ran while one was open for 0% of the time, Pallas kernels for 15%

profile of v4, /device:TPU:8, one launch (start us, length us, event | category | flops | bytes accessed | tf_op | source)
XLA Modules:
  0.0 67.1 jit_solution(12603247465631962263)
XLA Ops:
  0.6 0.0 copy-start
  0.6 2.0 %shard_map.121 = bf16[32,16,640]{2,1,0:T(8,128)(2,1)} custom-call(bf16[4,16,3072]{2,1,0:T(8,128)(2,1)} %projected.1, bf16[32,128]{1,0:T(8,128)(2,1)} %w_out.1), custom_call_target="tpu_custom_call" | custom-call | tf_op jit(solution)/shard_map/pallas_call | solution.py:236
  2.6 31.8 %all_to_all.10 = bf16[32,16,640]{2,1,0:T(8,128)(2,1)S(1)} all-to-all(bf16[32,16,640]{2,1,0:T(8,128)(2,1)} %shard_map.121), channel_id=1, replica_groups=mesh['gx'=8,'gy'=32] {'gy'}, dimensions={0} | all-to-all | bytes 1310720 | tf_op jit(solution)/shard_map/all_to_all | solution.py:309
  34.4 0.0 copy-start.1
  34.4 0.5 collective-permute-start.1
  34.9 1.6 %collective-permute-start = (bf16[32,16,256]{2,1,0:T(8,128)(2,1)S(1)}, bf16[32,16,256]{2,1,0:T(8,128)(2,1)S(1)}, u32[]{:S(2)}, u32[]{:S(2)}) collective-permute-start(bf16[32,16,256]{2,1,0:T(8,128)(2,1)S(1)} %slice.4.rest_0_), channel_id=1, source_target_pairs={{0,64},{32,96},{64,128},{96,160},{128,192},{160,224},{192,0},{224,... | collective-permute-start | bytes 786440 | tf_op jit(solution)/shard_map/ppermute | solution.py:317
  36.5 0.0 collective-permute-start.3
  36.5 0.0 copy-done.1
  36.5 10.4 %shard_map.122 = (bf16[512,128]{1,0:T(8,128)(2,1)}, f32[1,128,128]{2,1,0:T(8,128)}, f32[1,128,128]{2,1,0:T(8,128)}) custom-call(s32[4,64]{1,0:T(4,128)} %table_hbm.1, s32[4]{0:T(128)} %lengths_hbm.1, f32[3,1,8]{2,1,0:T(1,128)} %bitcast.7, bf16[512,640]{1,0:T(8,128)(2,1)} %bitcast.5, bf16[2,16,1024]{2,1,0:T(8,128)(2,1)} %persistent.1, ...), custom_call_target="tpu_custom_call" | custom-call | tf_op jit(solution)/shard_map/pallas_call | solution.py:190
  46.9 0.0 collective-permute-done.1.refs_1_
  46.9 0.0 collective-permute-done.refs_0_
  46.9 0.1 collective-permute-start.6
  47.0 0.1 collective-permute-start.5
  47.1 0.4 collective-permute-start.4
  47.5 0.6 collective-permute-start.2
  48.1 17.8 %all_to_all.11 = bf16[32,16,128]{2,1,0:T(8,128)(2,1)S(1)} all-to-all(bf16[32,16,128]{2,1,0:T(8,128)(2,1)} %bitcast.6), channel_id=1, replica_groups=mesh['gx'=8,'gy'=32] {'gy'}, dimensions={0} | all-to-all | bytes 262144 | tf_op jit(solution)/shard_map/all_to_all | solution.py:329
  65.9 0.0 collective-permute-done.3.rest_4_
  65.9 0.0 collective-permute-done.6.rest_7_
  65.9 0.0 collective-permute-done.5.rest_6_
  65.9 0.0 collective-permute-done.4.rest_5_
  65.9 0.0 collective-permute-done.2.rest_2_
  65.9 0.0 copy-done
  66.0 1.1 %shard_map.124 = bf16[4,16,1024]{2,1,0:T(8,128)(2,1)} custom-call(bf16[4,8,16,128]{3,2,1,0:T(8,128)(2,1)S(1)} %bitcast.4, bf16[32,16,256]{2,1,0:T(8,128)(2,1)S(1)} %slice.4.rest_0_, bf16[32,16,256]{2,1,0:T(8,128)(2,1)S(1)} %get-tuple-element.11.rest_1_, bf16[32,16,256]{2,1,0:T(8,128)(2,1)S(1)} %collective-permute-done.2.rest_2_, ...), custom_call_target="tpu_custom_call" | custom-call | tf_op jit(solution)/shard_map/pallas_call | solution.py:270
  (2 shorter events, 0.0 us)
Async XLA Ops:
  0.6 65.3 %copy-start = (bf16[4,16,1024]{2,1,0:T(8,128)(2,1)S(1)}, bf16[4,16,1024]{2,1,0:T(8,128)(2,1)}, u32[]{:S(2)}) copy-start(bf16[4,16,1024]{2,1,0:T(8,128)(2,1)} %rest_8_.1) | copy-start | bytes 393220
  34.4 2.1 %copy-start.1 = (bf16[32,16,640]{2,1,0:T(8,128)(2,1)}, bf16[32,16,640]{2,1,0:T(8,128)(2,1)S(1)}, u32[]{:S(2)}) copy-start(bf16[32,16,640]{2,1,0:T(8,128)(2,1)S(1)} %all_to_all.10) | copy-start | bytes 1966084
  34.4 12.5 %collective-permute-start.1 = (bf16[32,16,256]{2,1,0:T(8,128)(2,1)S(1)}, bf16[32,16,256]{2,1,0:T(8,128)(2,1)S(1)}, u32[]{:S(2)}, u32[]{:S(2)}) collective-permute-start(bf16[32,16,256]{2,1,0:T(8,128)(2,1)S(1)} %slice.4.rest_0_), channel_id=1, source_target_pairs={{0,192},{32,224},{64,0},{96,32},{128,64},{160,96},{192,128},{224,1... | collective-permute-start | bytes 786440 | tf_op jit(solution)/shard_map/ppermute | solution.py:317
  34.9 12.0 %collective-permute-start = (bf16[32,16,256]{2,1,0:T(8,128)(2,1)S(1)}, bf16[32,16,256]{2,1,0:T(8,128)(2,1)S(1)}, u32[]{:S(2)}, u32[]{:S(2)}) collective-permute-start(bf16[32,16,256]{2,1,0:T(8,128)(2,1)S(1)} %slice.4.rest_0_), channel_id=1, source_target_pairs={{0,64},{32,96},{64,128},{96,160},{128,192},{160,224},{192,0},{224,... | collective-permute-start | bytes 786440 | tf_op jit(solution)/shard_map/ppermute | solution.py:317
  36.5 29.4 %collective-permute-start.3 = (bf16[32,16,256]{2,1,0:T(8,128)(2,1)S(1)}, bf16[32,16,256]{2,1,0:T(8,128)(2,1)S(1)}, u32[]{:S(2)}, u32[]{:S(2)}) collective-permute-start(bf16[32,16,256]{2,1,0:T(8,128)(2,1)S(1)} %slice.4.rest_0_), channel_id=1, source_target_pairs={{0,32},{32,0},{64,96},{96,64},{128,160},{160,128},{192,224},{224,1... | collective-permute-start | bytes 786440 | tf_op jit(solution)/shard_map/ppermute | solution.py:318
  46.9 19.0 %collective-permute-start.6 = (bf16[32,16,256]{2,1,0:T(8,128)(2,1)S(1)}, bf16[32,16,256]{2,1,0:T(8,128)(2,1)S(1)}, u32[]{:S(2)}, u32[]{:S(2)}) collective-permute-start(bf16[32,16,256]{2,1,0:T(8,128)(2,1)S(1)} %get-tuple-element.12.rest_3_), channel_id=1, source_target_pairs={{0,32},{32,0},{64,96},{96,64},{128,160},{160,128},{192,224},{224,1... | collective-permute-start | bytes 786440 | tf_op jit(solution)/shard_map/ppermute | solution.py:335
  47.0 18.9 %collective-permute-start.5 = (bf16[32,16,256]{2,1,0:T(8,128)(2,1)S(1)}, bf16[32,16,256]{2,1,0:T(8,128)(2,1)S(1)}, u32[]{:S(2)}, u32[]{:S(2)}) collective-permute-start(bf16[32,16,256]{2,1,0:T(8,128)(2,1)S(1)} %get-tuple-element.11.rest_1_), channel_id=1, source_target_pairs={{0,96},{32,64},{64,160},{96,128},{128,224},{160,192},{192,32},{224... | collective-permute-start | bytes 786440 | tf_op jit(solution)/shard_map/ppermute | solution.py:334
  47.1 18.8 %collective-permute-start.4 = (bf16[32,16,256]{2,1,0:T(8,128)(2,1)S(1)}, bf16[32,16,256]{2,1,0:T(8,128)(2,1)S(1)}, u32[]{:S(2)}, u32[]{:S(2)}) collective-permute-start(bf16[32,16,256]{2,1,0:T(8,128)(2,1)S(1)} %get-tuple-element.11.rest_1_), channel_id=1, source_target_pairs={{0,32},{32,0},{64,96},{96,64},{128,160},{160,128},{192,224},{224,1... | collective-permute-start | bytes 786440 | tf_op jit(solution)/shard_map/ppermute | solution.py:335
  47.5 18.4 %collective-permute-start.2 = (bf16[32,16,256]{2,1,0:T(8,128)(2,1)S(1)}, bf16[32,16,256]{2,1,0:T(8,128)(2,1)S(1)}, u32[]{:S(2)}, u32[]{:S(2)}) collective-permute-start(bf16[32,16,256]{2,1,0:T(8,128)(2,1)S(1)} %get-tuple-element.11.rest_1_), channel_id=1, source_target_pairs={{0,64},{32,96},{64,128},{96,160},{128,192},{160,224},{192,0},{224,... | collective-permute-start | bytes 786440 | tf_op jit(solution)/shard_map/ppermute | solution.py:333

commit v5 on v4

--- a/solution.py
+++ b/solution.py
@@ -217,27 +217,48 @@
     )(table, lengths, rates, arrived, persistent, memory, moment, pages)
 
 
-def pack_kernel(projected, w_out, packed):
-    for request in range(packed.shape[0] // HEADS):
+def pack_kernel(projected, w_out, packed, held, weights, built, sems):
+    groups = held.shape[0]
+    incoming = [pltpu.make_async_copy(w_out, weights, sems.at[0])] + [
+        pltpu.make_async_copy(projected.at[r], held.at[r], sems.at[1 + r]) for r in range(groups)
+    ]
+    for copy in incoming:
+        copy.start()
+    incoming[0].wait()
+    columns = jnp.concatenate([weights[:16, :], weights[16:, :]], 1)
+    outgoing = []
+    for r in range(groups):
+        incoming[1 + r].wait()
         for head in range(HEADS):
+            member = r * HEADS + head
             for part in range(3):
                 start = part * D + head * HD
-                packed[request * HEADS + head, :, part * HD : (part + 1) * HD] = projected[
-                    request, :, start : start + HD
-                ]
-    weights = jnp.concatenate([w_out[:16, :], w_out[16:, :]], 1)
-    for member in range(packed.shape[0]):
-        packed[member, :, 3 * HD :] = weights
+                built[member, :, part * HD : (part + 1) * HD] = held[r, :, start : start + HD]
+            built[member, :, 3 * HD :] = columns
+        mine = pl.ds(r * HEADS, HEADS)
+        copy = pltpu.make_async_copy(built.at[mine], packed.at[mine], sems.at[1 + groups + r])
+        copy.start()
+        outgoing.append(copy)
+    for copy in outgoing:
+        copy.wait()
 
 
 def pack_call(projected, w_out):
-    vmem = pl.BlockSpec(memory_space=pltpu.VMEM)
+    hbm = pl.BlockSpec(memory_space=pltpu.HBM)
     groups, positions, _ = projected.shape
+    shape = (groups * HEADS, positions, 5 * HD)
     return pl.pallas_call(
         pack_kernel,
-        out_shape=jax.ShapeDtypeStruct((groups * HEADS, positions, 5 * HD), bf),
-        in_specs=[vmem, vmem],
-        out_specs=vmem,
+        out_shape=jax.ShapeDtypeStruct(shape, bf),
+        in_specs=[hbm, hbm],
+        out_specs=hbm,
+        scratch_shapes=[
+            pltpu.VMEM(projected.shape, bf),
+            pltpu.VMEM(w_out.shape, bf),
+            pltpu.VMEM(shape, bf),
+            pltpu.SemaphoreType.DMA((1 + 2 * groups,)),
+        ],
+        compiler_params=pltpu.CompilerParams(vmem_limit_bytes=60 << 20),
     )(projected, w_out)
 
 
@@ -331,10 +352,10 @@
     )
     below, above, memory_next = hold_call([below, above, memory_next])
     far = lax.ppermute(below, "gx", along[1])
-    diagonal = lax.ppermute(below, "gx", [(i, j ^ 1) for i, j in along[1]])
     near = [lax.ppermute(block, "gx", across) for block in (below, above)]
+    returned, far = lax.optimization_barrier((returned, far))
     blocks = [own, below, far, above]
-    others = [beside, near[0], diagonal, near[1]]
+    others = [beside, near[0], lax.ppermute(far, "gx", across), near[1]]
     layer_out = project_call(
         returned.reshape(groups, HEADS, positions, HD), blocks + others, residual
     )

time: 67.8 us -> 67.7 us (level)
  the two profiles are of different devices: /device:TPU:8 before, /device:TPU:1 now
where the time goes in v5:
time: 67.7 us; the launch traced here: 67.2 us
  blocking collectives  28.3 us (42%)
  starting transfers between devices  20.7 us (31%)
  Pallas kernels  9.81 us (14%)
  waiting for transfers between devices  7.72 us (11%)
  between operations  0.7 us (1%)
    all_to_all x1, blocking collectives, shards(): lax.all_to_all(packed, 'gy', split_axis=0, concat_axis=0, tiled=True)  28.3 us
    all_to_all x1, starting transfers between devices, shards(): lax.all_to_all(mixed.reshape(groups * HEADS, positions, HD), 'gy', split_...  8.4 us
    pallas_call x1, Pallas kernels, pair_call(): pl.pallas_call(pair_kernel, out_shape=(jax.ShapeDtypeStruct((ROWS, HD), b...  6.78 us
    all_to_all x1, waiting for transfers between devices, shards(): lax.all_to_all(mixed.reshape(groups * HEADS, positions, HD), 'gy', split_...  6.55 us
    ppermute x1, starting transfers between devices, shards(): far = lax.ppermute(below, 'gx', along[1])  3.68 us
    ppermute x1, starting transfers between devices, shards(): others = [beside, near[0], lax.ppermute(far, 'gx', across), near[1]]  3.22 us
    ppermute x2, starting transfers between devices, shards(): below, above = [lax.ppermute(own, 'gx', along[k]) for k in (1, chips - 1)]  2.81 us
    ppermute x1, starting transfers between devices, shards(): beside = lax.ppermute(own, 'gx', across)  2.09 us
  transfers between devices with their start and end apart: 8, of which 2 were waited for; matrix products, arithmetic and copies ran while one was open for 0% of the time, Pallas kernels for 10%

profile of v5, /device:TPU:1, one launch (start us, length us, event | category | flops | bytes accessed | tf_op | source)
XLA Modules:
  0.0 67.2 jit_solution(5524785833764819248)
XLA Ops:
  0.6 0.0 copy-start
  0.6 1.9 %shard_map.121 = bf16[32,16,640]{2,1,0:T(8,128)(2,1)} custom-call(bf16[4,16,3072]{2,1,0:T(8,128)(2,1)} %projected.1, bf16[32,128]{1,0:T(8,128)(2,1)} %w_out.1), custom_call_target="tpu_custom_call" | custom-call | tf_op jit(solution)/shard_map/pallas_call | solution.py:250
  2.5 28.3 %all_to_all.10 = bf16[32,16,640]{2,1,0:T(8,128)(2,1)S(1)} all-to-all(bf16[32,16,640]{2,1,0:T(8,128)(2,1)} %shard_map.121), channel_id=1, replica_groups=mesh['gx'=8,'gy'=32] {'gy'}, dimensions={0} | all-to-all | bytes 1310720 | tf_op jit(solution)/shard_map/all_to_all | solution.py:330
  30.8 0.0 copy-start.1
  30.8 2.8 %collective-permute-start.1 = (bf16[32,16,256]{2,1,0:T(8,128)(2,1)S(1)}, bf16[32,16,256]{2,1,0:T(8,128)(2,1)S(1)}, u32[]{:S(2)}, u32[]{:S(2)}) collective-permute-start(bf16[32,16,256]{2,1,0:T(8,128)(2,1)S(1)} %slice.4.rest_0_), channel_id=1, source_target_pairs={{0,192},{32,224},{64,0},{96,32},{128,64},{160,96},{192,128},{224,1... | collective-permute-start | bytes 786440 | tf_op jit(solution)/shard_map/ppermute | solution.py:338
  33.6 0.0 collective-permute-start
  33.6 0.0 copy-done.1
  33.6 6.8 %shard_map.122 = (bf16[512,128]{1,0:T(8,128)(2,1)}, f32[1,128,128]{2,1,0:T(8,128)}, f32[1,128,128]{2,1,0:T(8,128)}) custom-call(s32[4,64]{1,0:T(4,128)} %table_hbm.1, s32[4]{0:T(128)} %lengths_hbm.1, f32[3,1,8]{2,1,0:T(1,128)} %bitcast.7, bf16[512,640]{1,0:T(8,128)(2,1)} %bitcast.5, bf16[2,16,1024]{2,1,0:T(8,128)(2,1)} %persistent.1, ...), custom_call_target="tpu_custom_call" | custom-call | tf_op jit(solution)/shard_map/pallas_call | solution.py:190
  40.4 0.0 collective-permute-done.1.refs_1_
  40.4 0.0 collective-permute-done.refs_0_
  40.5 3.7 %collective-permute-start.2 = (bf16[32,16,256]{2,1,0:T(8,128)(2,1)S(1)}, bf16[32,16,256]{2,1,0:T(8,128)(2,1)S(1)}, u32[]{:S(2)}, u32[]{:S(2)}) collective-permute-start(bf16[32,16,256]{2,1,0:T(8,128)(2,1)S(1)} %get-tuple-element.13.rest_1_), channel_id=1, source_target_pairs={{0,64},{32,96},{64,128},{96,160},{128,192},{160,224},{192,0},{224,... | collective-permute-start | bytes 786440 | tf_op jit(solution)/shard_map/ppermute | solution.py:354
  44.1 8.4 %all-to-all-start.1 = ((bf16[32,16,128]{2,1,0:T(8,128)(2,1)}), bf16[32,16,128]{2,1,0:T(8,128)(2,1)S(1)}, u32[]{:S(2)}, u32[]{:S(2)}) async-start(bf16[32,16,128]{2,1,0:T(8,128)(2,1)} %bitcast.6), calls=%async_computation.1 | async-start | bytes 262144 | tf_op jit(solution)/shard_map/all_to_all | solution.py:350
  52.5 2.1 %collective-permute-start.3 = (bf16[32,16,256]{2,1,0:T(8,128)(2,1)S(1)}, bf16[32,16,256]{2,1,0:T(8,128)(2,1)S(1)}, u32[]{:S(2)}, u32[]{:S(2)}) collective-permute-start(bf16[32,16,256]{2,1,0:T(8,128)(2,1)S(1)} %slice.4.rest_0_), channel_id=1, source_target_pairs={{0,32},{32,0},{64,96},{96,64},{128,160},{160,128},{192,224},{224,1... | collective-permute-start | bytes 786440 | tf_op jit(solution)/shard_map/ppermute | solution.py:339
  54.6 0.1 collective-permute-start.4
  54.7 0.4 collective-permute-start.6
  55.1 6.6 %all-to-all-done.1 = bf16[32,16,128]{2,1,0:T(8,128)(2,1)S(1)} async-done(((bf16[32,16,128]{2,1,0:T(8,128)(2,1)}), bf16[32,16,128]{2,1,0:T(8,128)(2,1)S(1)}, u32[]{:S(2)}, u32[]{:S(2)}) %all-to-all-start.1) | async-done | bytes 131104 | tf_op jit(solution)/shard_map/all_to_all | solution.py:350
  61.7 0.0 collective-permute-done.2.rest_2_
  61.7 3.2 %collective-permute-start.5 = (bf16[32,16,256]{2,1,0:T(8,128)(2,1)S(1)}, bf16[32,16,256]{2,1,0:T(8,128)(2,1)S(1)}, u32[]{:S(2)}, u32[]{:S(2)}) collective-permute-start(bf16[32,16,256]{2,1,0:T(8,128)(2,1)S(1)} %collective-permute-done.2.rest_2_), channel_id=1, source_target_pairs={{0,32},{32,0},{64,96},{96,64},{128,160},{160,128},{192,224},{224,1... | collective-permute-start | bytes 786440 | tf_op jit(solution)/shard_map/ppermute | solution.py:358
  64.9 0.0 collective-permute-done.3.rest_4_
  64.9 0.0 collective-permute-done.6.rest_7_
  64.9 0.0 collective-permute-done.4.rest_5_
  64.9 1.1 %collective-permute-done.5.rest_6_ = bf16[32,16,256]{2,1,0:T(8,128)(2,1)S(1)} collective-permute-done((bf16[32,16,256]{2,1,0:T(8,128)(2,1)S(1)}, bf16[32,16,256]{2,1,0:T(8,128)(2,1)S(1)}, u32[]{:S(2)}, u32[]{:S(2)}) %collective-permute-start.5) | collective-permute-done | bytes 262176 | tf_op jit(solution)/shard_map/ppermute | solution.py:358
  66.1 0.0 copy-done
  66.1 1.1 %shard_map.124 = bf16[4,16,1024]{2,1,0:T(8,128)(2,1)} custom-call(bf16[4,8,16,128]{3,2,1,0:T(8,128)(2,1)S(1)} %bitcast.4, bf16[32,16,256]{2,1,0:T(8,128)(2,1)S(1)} %slice.4.rest_0_, bf16[32,16,256]{2,1,0:T(8,128)(2,1)S(1)} %get-tuple-element.13.rest_1_, bf16[32,16,256]{2,1,0:T(8,128)(2,1)S(1)} %collective-permute-done.2.rest_2_, ...), custom_call_target="tpu_custom_call" | custom-call | tf_op jit(solution)/shard_map/pallas_call | solution.py:291
  (2 shorter events, 0.0 us)
Async XLA Ops:
  0.6 65.5 %copy-start = (bf16[4,16,1024]{2,1,0:T(8,128)(2,1)S(1)}, bf16[4,16,1024]{2,1,0:T(8,128)(2,1)}, u32[]{:S(2)}) copy-start(bf16[4,16,1024]{2,1,0:T(8,128)(2,1)} %rest_8_.1) | copy-start | bytes 393220
  30.8 2.8 %copy-start.1 = (bf16[32,16,640]{2,1,0:T(8,128)(2,1)}, bf16[32,16,640]{2,1,0:T(8,128)(2,1)S(1)}, u32[]{:S(2)}) copy-start(bf16[32,16,640]{2,1,0:T(8,128)(2,1)S(1)} %all_to_all.10) | copy-start | bytes 1966084
  30.8 9.6 %collective-permute-start.1 = (bf16[32,16,256]{2,1,0:T(8,128)(2,1)S(1)}, bf16[32,16,256]{2,1,0:T(8,128)(2,1)S(1)}, u32[]{:S(2)}, u32[]{:S(2)}) collective-permute-start(bf16[32,16,256]{2,1,0:T(8,128)(2,1)S(1)} %slice.4.rest_0_), channel_id=1, source_target_pairs={{0,192},{32,224},{64,0},{96,32},{128,64},{160,96},{192,128},{224,1... | collective-permute-start | bytes 786440 | tf_op jit(solution)/shard_map/ppermute | solution.py:338
  33.6 6.8 %collective-permute-start = (bf16[32,16,256]{2,1,0:T(8,128)(2,1)S(1)}, bf16[32,16,256]{2,1,0:T(8,128)(2,1)S(1)}, u32[]{:S(2)}, u32[]{:S(2)}) collective-permute-start(bf16[32,16,256]{2,1,0:T(8,128)(2,1)S(1)} %slice.4.rest_0_), channel_id=1, source_target_pairs={{0,64},{32,96},{64,128},{96,160},{128,192},{160,224},{192,0},{224,... | collective-permute-start | bytes 786440 | tf_op jit(solution)/shard_map/ppermute | solution.py:338
  40.5 21.2 %collective-permute-start.2 = (bf16[32,16,256]{2,1,0:T(8,128)(2,1)S(1)}, bf16[32,16,256]{2,1,0:T(8,128)(2,1)S(1)}, u32[]{:S(2)}, u32[]{:S(2)}) collective-permute-start(bf16[32,16,256]{2,1,0:T(8,128)(2,1)S(1)} %get-tuple-element.13.rest_1_), channel_id=1, source_target_pairs={{0,64},{32,96},{64,128},{96,160},{128,192},{160,224},{192,0},{224,... | collective-permute-start | bytes 786440 | tf_op jit(solution)/shard_map/ppermute | solution.py:354
  44.1 17.6 %all-to-all-start.1 = ((bf16[32,16,128]{2,1,0:T(8,128)(2,1)}), bf16[32,16,128]{2,1,0:T(8,128)(2,1)S(1)}, u32[]{:S(2)}, u32[]{:S(2)}) async-start(bf16[32,16,128]{2,1,0:T(8,128)(2,1)} %bitcast.6), calls=%async_computation.1 | async-start | bytes 262144 | tf_op jit(solution)/shard_map/all_to_all | solution.py:350
  52.5 12.4 %collective-permute-start.3 = (bf16[32,16,256]{2,1,0:T(8,128)(2,1)S(1)}, bf16[32,16,256]{2,1,0:T(8,128)(2,1)S(1)}, u32[]{:S(2)}, u32[]{:S(2)}) collective-permute-start(bf16[32,16,256]{2,1,0:T(8,128)(2,1)S(1)} %slice.4.rest_0_), channel_id=1, source_target_pairs={{0,32},{32,0},{64,96},{96,64},{128,160},{160,128},{192,224},{224,1... | collective-permute-start | bytes 786440 | tf_op jit(solution)/shard_map/ppermute | solution.py:339
  54.6 10.3 %collective-permute-start.4 = (bf16[32,16,256]{2,1,0:T(8,128)(2,1)S(1)}, bf16[32,16,256]{2,1,0:T(8,128)(2,1)S(1)}, u32[]{:S(2)}, u32[]{:S(2)}) collective-permute-start(bf16[32,16,256]{2,1,0:T(8,128)(2,1)S(1)} %get-tuple-element.13.rest_1_), channel_id=1, source_target_pairs={{0,32},{32,0},{64,96},{96,64},{128,160},{160,128},{192,224},{224,1... | collective-permute-start | bytes 786440 | tf_op jit(solution)/shard_map/ppermute | solution.py:355
  54.7 10.2 %collective-permute-start.6 = (bf16[32,16,256]{2,1,0:T(8,128)(2,1)S(1)}, bf16[32,16,256]{2,1,0:T(8,128)(2,1)S(1)}, u32[]{:S(2)}, u32[]{:S(2)}) collective-permute-start(bf16[32,16,256]{2,1,0:T(8,128)(2,1)S(1)} %get-tuple-element.16.rest_3_), channel_id=1, source_target_pairs={{0,32},{32,0},{64,96},{96,64},{128,160},{160,128},{192,224},{224,1... | collective-permute-start | bytes 786440 | tf_op jit(solution)/shard_map/ppermute | solution.py:355
  61.7 4.4 %collective-permute-start.5 = (bf16[32,16,256]{2,1,0:T(8,128)(2,1)S(1)}, bf16[32,16,256]{2,1,0:T(8,128)(2,1)S(1)}, u32[]{:S(2)}, u32[]{:S(2)}) collective-permute-start(bf16[32,16,256]{2,1,0:T(8,128)(2,1)S(1)} %collective-permute-done.2.rest_2_), channel_id=1, source_target_pairs={{0,32},{32,0},{64,96},{96,64},{128,160},{160,128},{192,224},{224,1... | collective-permute-start | bytes 786440 | tf_op jit(solution)/shard_map/ppermute | solution.py:358
